TPU v7x, 32 devices: a whole 2x2x4 slice. The times are simulated.
32 devices in a mesh: section: 4 (over y, x), coil: 4 (over z), cuts: 2 (over core).
Axes of the slice: x: 2, y: 2, z: 4, core: 2. Of those that a mesh axis runs over, the one named last changes fastest.
Arguments:
- initial: bfloat16 [2, 32, 80, 2, 128], P(None, 'coil', 'cuts'), may hold values from -6 to 6
- sens: bfloat16 [2, 8, 32, 80, 2, 128], P(None, ('coil', 'cuts')), may hold values from -2.5 to 2.5
- kspace: bfloat16 [2, 8, 32, 80, 2, 128], P(None, ('coil', 'cuts')), may hold values from -6 to 6
- mask: int32 [2, 80, 128], replicated, may hold values 0 or 1
- step_sizes: float32 [4], P('section'), may hold values from 0.3 to 1.5
- conv_in: bfloat16 [4, 128, 18], P('section'), may hold values from -1.5 to 1.5
- bias_in: float32 [4, 128], P('section'), may hold values from -3 to 3
- conv_out: bfloat16 [4, 18, 128], P('section'), may hold values from -0.1875 to 0.1875
Outputs:
- cascade_images: bfloat16 [4, 2, 32, 80, 2, 128], P('section', None, 'coil', 'cuts')
Inputs may be any that keep to these rules, and one draw needn't show every extreme that they name: `mask`: 1 marks a sampled phase-encoding line of the slab, 0 one that was not measured.
All inputs are finite; a program needn't handle non-finite values.
Results may differ from a plain program's by a relative error of at most 0.028.
Values may be sent and summed in bfloat16 or wider, within the bound.
No kernel may reach another device: no remote copies, remote signals or barrier semaphores. Data moves between devices by JAX's collectives and lax.ppermute only.
A program may use at most 128 MiB of HBM per device.

v0:
```python
import math
import jax
import jax.numpy as jnp
from jax import lax
from jax.sharding import PartitionSpec as P


def extended_2(x, sides, width):
    for axis, dim in sides:
        size, length = (lax.axis_size(axis), x.shape[dim])
        up = [(i, (i + 1) % size) for i in range(size - 1)]
        down = [(j, i) for i, j in up]
        last = lax.slice_in_dim(x, length - width, length, axis=dim)
        leading = lax.slice_in_dim(x, 0, width, axis=dim)
        before = lax.ppermute(last, axis, up)
        after = lax.ppermute(leading, axis, down)
        x = jnp.concatenate([before, x, after], axis=dim)
    return x


def from_partner(block, axis, bit):
    count = lax.axis_size(axis)
    route = []
    for low in range(count):
        high = low | 1 << bit
        if high != low and high < count:
            route += [(low, high), (high, low)]
    return lax.ppermute(block, axis, route)


def dft_table(length, sign):
    ramp = jnp.arange(length, dtype=jnp.int32)
    phase = ramp[:, None] * ramp[None, :] % length
    angle = phase.astype(jnp.float32) * (2.0 * math.pi / length)
    scale = 1.0 / math.sqrt(length)
    cosine = jnp.cos(angle) * scale
    sine = jnp.sin(angle) * (scale * sign)
    upper = jnp.concatenate([cosine, -sine], axis=1)
    lower = jnp.concatenate([sine, cosine], axis=1)
    return jnp.concatenate([upper, lower], axis=0).astype(jnp.bfloat16)


def pass_last(volume, table):
    shape = volume.shape
    flat = volume.reshape(-1, shape[-2] * shape[-1])
    return (
        jnp.dot(flat, table, preferred_element_type=jnp.float32).astype(jnp.bfloat16).reshape(shape)
    )


def pass_middle(volume, table):
    length = volume.shape[1]
    split = table.reshape(2, length, 2, length)
    return jnp.einsum("pjcz,cjdk->pkdz", volume, split, preferred_element_type=jnp.float32).astype(
        jnp.bfloat16
    )


def pass_first(volume, table):
    length = volume.shape[0]
    split = table.reshape(2, length, 2, length)
    return jnp.einsum("jycz,cjdk->kydz", volume, split, preferred_element_type=jnp.float32).astype(
        jnp.bfloat16
    )


def complex_product(sens, image):
    sens_real = sens[:, :, 0].astype(jnp.float32)
    sens_imag = sens[:, :, 1].astype(jnp.float32)
    image_real = image[:, :, 0].astype(jnp.float32)
    image_imag = image[:, :, 1].astype(jnp.float32)
    return jnp.stack(
        [
            sens_real * image_real - sens_imag * image_imag,
            sens_real * image_imag + sens_imag * image_real,
        ],
        axis=2,
    )


def conj_product(sens, back):
    sens_real = sens[:, :, 0].astype(jnp.float32)
    sens_imag = sens[:, :, 1].astype(jnp.float32)
    back_real = back[:, :, 0].astype(jnp.float32)
    back_imag = back[:, :, 1].astype(jnp.float32)
    return jnp.stack(
        [
            sens_real * back_real + sens_imag * back_imag,
            sens_real * back_imag - sens_imag * back_real,
        ],
        axis=2,
    )


def hidden_layer(extended, out_rows, weights_in, bias):
    width = extended.shape[3]
    padded = jnp.pad(extended, ((0, 0), (0, 0), (0, 0), (1, 1)))
    taps = jnp.stack(
        [
            padded[:, shift_row : shift_row + out_rows, :, shift_col : shift_col + width]
            for shift_row in range(3)
            for shift_col in range(3)
        ],
        axis=2,
    )
    taps = taps.reshape(extended.shape[0], out_rows, 18, width)
    summed = jnp.einsum("hf,xyfz->xyhz", weights_in, taps, preferred_element_type=jnp.float32)
    return jax.nn.silu(summed + bias[None, None, :, None]).astype(jnp.bfloat16)


def combine_taps(beside_all, rows):
    width = beside_all.shape[3]
    padded = jnp.pad(beside_all, ((0, 0), (0, 0), (0, 0), (1, 1)))
    total = jnp.zeros((beside_all.shape[0], rows, 2, width), jnp.float32)
    for shift_row in range(3):
        for shift_col in range(3):
            first = (3 * shift_row + shift_col) * 2
            total = (
                total
                + padded[
                    :,
                    shift_row : shift_row + rows,
                    first : first + 2,
                    shift_col : shift_col + width,
                ]
            )
    return total


def refine_rows(current, weights_in, bias, weights_out):
    rows = current.shape[1]
    extended = extended_2(current, (("cuts", 1),), 1)
    hidden = hidden_layer(extended, rows, weights_in, bias)
    product = jnp.einsum("fh,xyhz->xyfz", weights_out, hidden, preferred_element_type=jnp.float32)
    beside_all = extended_2(product.astype(jnp.bfloat16), (("cuts", 1),), 1).astype(product.dtype)
    return combine_taps(beside_all, rows)


def whole_rows(current):
    return lax.all_gather(current, "cuts", axis=1, tiled=True)


def sum_gradient(back_rows, current):
    mine = lax.psum_scatter(
        back_rows(jnp.int32(0), lax.axis_size("coil") * current.shape[0]).astype(jnp.bfloat16),
        "coil",
        scatter_dimension=0,
        tiled=True,
    )
    grad = lax.psum_scatter(mine, "cuts", scatter_dimension=1, tiled=True).astype(jnp.float32)
    return grad


def finish_step(current, grad, step, weights_in, bias, weights_out):
    refine = refine_rows(current, weights_in, bias, weights_out)
    return (current.astype(jnp.float32) - step * grad + refine).astype(jnp.bfloat16)


def pair_block(current, sens_one, data_one, mask_one, step, weights_in, bias, weights_out, half):
    halves = whole_rows(current)
    whole = lax.all_gather(halves, "coil", axis=0, tiled=True)
    size_x, size_y, _, size_z = whole.shape
    half_x = size_x // 2
    half_y = size_y // 2
    forward_x, forward_y, forward_z = (
        dft_table(size_x, 1.0),
        dft_table(size_y, 1.0),
        dft_table(size_z, 1.0),
    )
    back_x, back_y, back_z = (
        dft_table(size_x, -1.0),
        dft_table(size_y, -1.0),
        dft_table(size_z, -1.0),
    )
    lower_side = half == 0
    x_start = half * half_x
    x_other = (1 - half) * half_x
    y_start = half * half_y
    y_other = (1 - half) * half_y
    rows_in = lax.dynamic_slice_in_dim(whole, x_start, half_x, 0)
    sens_rows = lax.dynamic_slice_in_dim(sens_one, x_start, half_x, 0)
    coil_image = complex_product(sens_rows, rows_in).astype(jnp.bfloat16)
    partial_value = pass_middle(pass_last(coil_image, forward_z), forward_y)
    kept = lax.dynamic_slice_in_dim(partial_value, y_start, half_y, 1)
    sent = lax.dynamic_slice_in_dim(partial_value, y_other, half_y, 1)
    arrived = from_partner(sent, "section", 0)
    assembled = jnp.concatenate(
        [jnp.where(lower_side, kept, arrived), jnp.where(lower_side, arrived, kept)], axis=0
    )
    predicted = pass_first(assembled, forward_x)
    data_half = lax.dynamic_slice_in_dim(data_one, y_start, half_y, 1)
    mask_half = lax.dynamic_slice_in_dim(mask_one, y_start, half_y, 0)
    weight_mask = mask_half.astype(jnp.float32)[None, :, None, :]
    resid = (weight_mask * (data_half.astype(jnp.float32) - predicted.astype(jnp.float32))).astype(
        jnp.bfloat16
    )
    spectrum = pass_first(resid, back_x)
    kept_back = lax.dynamic_slice_in_dim(spectrum, x_start, half_x, 0)
    sent_back = lax.dynamic_slice_in_dim(spectrum, x_other, half_x, 0)
    arrived_back = from_partner(sent_back, "section", 0)
    joined = jnp.concatenate(
        [
            jnp.where(lower_side, kept_back, arrived_back),
            jnp.where(lower_side, arrived_back, kept_back),
        ],
        axis=1,
    )
    back = pass_last(pass_middle(joined, back_y), back_z)
    term = conj_product(sens_rows, back)
    blank = jnp.zeros_like(term)
    full_term = jnp.concatenate(
        [jnp.where(lower_side, term, blank), jnp.where(lower_side, blank, term)], axis=0
    )

    def back_rows(start, count):
        return full_term

    grad = sum_gradient(back_rows, current)
    grad = grad + from_partner(grad.astype(jnp.bfloat16), "section", 0).astype(grad.dtype)
    return finish_step(current, grad, step, weights_in, bias, weights_out)


def body(initial, sens, kspace, mask, step_sizes, conv_in, bias_in, conv_out):
    section_count = lax.axis_size("section")
    position = lax.axis_index("section")
    all_steps, all_bias = (
        lax.all_gather(step_sizes, "section", axis=0, tiled=True),
        lax.all_gather(bias_in, "section", axis=0, tiled=True),
    )
    all_in, all_out = (
        lax.all_gather(conv_in, "section", axis=0, tiled=True),
        lax.all_gather(conv_out, "section", axis=0, tiled=True),
    )
    slab = position // 2
    half = position % 2
    current = lax.dynamic_index_in_dim(initial, slab, 0, keepdims=False)
    sens_one = lax.dynamic_index_in_dim(sens, slab, 0, keepdims=False)[0]
    data_one = lax.dynamic_index_in_dim(kspace, slab, 0, keepdims=False)[0]
    mask_one = lax.dynamic_index_in_dim(mask, slab, 0, keepdims=False)
    images = []
    for cascade in range(section_count):
        current = pair_block(
            current,
            sens_one,
            data_one,
            mask_one,
            all_steps[cascade],
            all_in[cascade],
            all_bias[cascade],
            all_out[cascade],
            half,
        )
        images.append(current)
    stacked = jnp.stack(images, axis=0)[:, None]
    arrived = lax.all_to_all(stacked, "section", split_axis=0, concat_axis=1, tiled=True)
    return arrived[:, ::2]


def solution(mesh):
    return jax.shard_map(
        body,
        mesh=mesh,
        in_specs=(
            P(None, "coil", "cuts", None, None),
            P(None, ("coil", "cuts"), None, None, None, None),
            P(None, ("coil", "cuts"), None, None, None, None),
            P(),
            P("section"),
            P("section", None, None),
            P("section", None),
            P("section", None, None),
        ),
        out_specs=P("section", None, "coil", "cuts", None, None),
        check_vma=False,
    )
```

profile of v0, /device:TPU:0, one launch (start us, length us, event | category | flops | bytes accessed | tf_op | source)
XLA Modules:
  0.0 516.5 jit_solution(3672511079097253560)
XLA Ops:
  7.8 2.3 all-gather
  12.5 32.9 %all-gather.14.cloned.1.call-done = bf16[1,32,80,2,128]{4,2,3,0,1:T(8,128)(2,1)} async-done(((bf16[1,8,80,2,128]{4,2,3,0,1:T(8,128)(2,1)}), bf16[1,32,80,2,128]{4,2,3,0,1:T(8,128)(2,1)}) %all-gather.14.cloned.1.call-update) | async-done | bytes 1310736 | tf_op jit(solution)/shard_map/all_gather | solution.py:161
  48.3 1.5 collective-permute-start
  51.0 1.6 constant_dynamic-slice_fusion
  52.6 4.5 collective-permute-done
  58.4 1.6 collective-permute-start.1
  60.5 5.9 %collective-permute-done.1 = bf16[16,40,2,128]{3,1,0,2:T(8,128)(2,1)S(1)} collective-permute-done((bf16[16,40,2,128]{3,1,0,2:T(8,128)(2,1)S(1)}, bf16[16,40,2,128]{3,1,0,2:T(8,128)(2,1)S(1)}, u32[]{:S(2)}, u32[]{:S(2)}) %collective-permute-start.1) | collective-permute-done | bytes 327712 | tf_op jit(solution)/shard_map/ppermute | solution.py:28
  75.5 7.9 %all-gather.2 = f32[4,1,128]{2,1,0:T(1,128)S(1)} all-gather(f32[1,1,128]{2,1,0:T(1,128)S(1)} %bitcast.665), channel_id=1, replica_groups=mesh['section'=4,'coil'=4,'cuts'=2] {'section'}, dimensions={0}, use_global_device_ids=true | all-gather | bytes 2560 | tf_op jit(solution)/shard_map/all_gather | solution.py:228
  83.4 8.1 %all_gather.39 = bf16[4,128,18]{1,2,0:T(8,128)(2,1)S(1)} all-gather(bf16[1,128,18]{1,2,0:T(8,128)(2,1)S(1)} %copy-done.37), channel_id=1, replica_groups=mesh['section'=4,'coil'=4,'cuts'=2] {'section'}, dimensions={0}, use_global_device_ids=true | all-gather | bytes 23040 | tf_op jit(solution)/shard_map/all_gather | solution.py:231
  91.5 8.9 %all-reduce.8 = f32[4]{0:T(128)S(1)} all-reduce(f32[4]{0:T(128)S(1)} %dynamic-update-slice), channel_id=1, replica_groups=mesh['section'=4,'coil'=4,'cuts'=2] {'section'}, use_global_device_ids=true, to_apply=%add.8 | all-reduce | flops 4 | bytes 32
  100.4 7.4 %all_gather.41 = bf16[4,18,128]{2,1,0:T(8,128)(2,1)S(1)} all-gather(bf16[1,18,128]{2,1,0:T(8,128)(2,1)S(1)} %copy-done.38), channel_id=1, replica_groups=mesh['section'=4,'coil'=4,'cuts'=2] {'section'}, dimensions={0}, use_global_device_ids=true | all-gather | bytes 23040 | tf_op jit(solution)/shard_map/all_gather | solution.py:232
  111.6 1.8 copy.168
  113.5 10.2 %convert_bitcast_fusion.3 = bf16[8,40,18,128]{3,2,1,0:T(8,128)(2,1)S(1)} fusion(f32[128]{0:T(128)S(1)} %get-tuple-element.73, bf16[8,40,18,128]{3,1,2,0:T(8,128)(2,1)} %bitcast.650, bf16[4,18,128]{2,1,0:T(8,128)(2,1)S(1)} %all_gather.41, bf16[4,128,18]{1,2,0:T(8,128)(2,1)S(1)} %all_gather.39), kind=kOutput, calls=%fused_computation.111 | convolution fusion | flops 409681920 | bytes 2961920 | tf_op jit(solution)/shard_map/fh,xyhz->xyfz/dot_general | solution.py:134
  125.1 1.7 collective-permute-start.6
  128.5 1.5 collective-permute-start.2
  130.5 5.0 collective-permute-done.2
  135.5 2.8 fusion.196
  138.2 2.0 all_gather.42
  141.1 32.4 %all-gather.8.cloned.1.call-done = bf16[32,80,2,128]{3,1,2,0:T(8,128)(2,1)} async-done(((bf16[8,80,2,128]{3,1,2,0:T(8,128)(2,1)}), bf16[32,80,2,128]{3,1,2,0:T(8,128)(2,1)}) %all-gather.8.cloned.1.call-update) | async-done | bytes 1310736 | tf_op jit(solution)/shard_map/all_gather | solution.py:161
  176.6 1.5 collective-permute-start.7
  178.1 7.3 %collective-permute-done.7 = bf16[16,40,2,128]{3,1,0,2:T(8,128)(2,1)S(1)} collective-permute-done((bf16[16,40,2,128]{3,1,0,2:T(8,128)(2,1)S(1)}, bf16[16,40,2,128]{3,1,0,2:T(8,128)(2,1)S(1)}, u32[]{:S(2)}, u32[]{:S(2)}) %collective-permute-start.7) | collective-permute-done | bytes 327712 | tf_op jit(solution)/shard_map/ppermute | solution.py:28
  186.8 1.5 collective-permute-start.8
  188.3 6.4 %collective-permute-done.8 = bf16[16,40,2,128]{3,1,0,2:T(8,128)(2,1)S(1)} collective-permute-done((bf16[16,40,2,128]{3,1,0,2:T(8,128)(2,1)S(1)}, bf16[16,40,2,128]{3,1,0,2:T(8,128)(2,1)S(1)}, u32[]{:S(2)}, u32[]{:S(2)}) %collective-permute-start.8) | collective-permute-done | bytes 327712 | tf_op jit(solution)/shard_map/ppermute | solution.py:28
  200.3 1.5 collective-permute-start.11
  201.8 1.6 collective-permute-done.11
  207.1 24.2 %reduce-scatter.13.cloned.1.call-done = bf16[8,80,2,128]{3,1,2,0:T(8,128)(2,1)} async-done(((bf16[32,80,2,128]{3,1,2,0:T(8,128)(2,1)}), bf16[8,80,2,128]{3,1,2,0:T(8,128)(2,1)}) %reduce-scatter.13.cloned.1.call-update) | async-done | bytes 327696 | tf_op jit(solution)/shard_map/reduce_scatter | solution.py:144
  231.2 1.8 copy.189
  233.1 10.2 %convert_bitcast_fusion.2 = bf16[8,40,18,128]{3,2,1,0:T(8,128)(2,1)S(1)} fusion(f32[128]{0:T(128)S(1)} %get-tuple-element.75, bf16[8,40,18,128]{3,1,2,0:T(8,128)(2,1)} %bitcast.651, bf16[4,18,128]{2,1,0:T(8,128)(2,1)} %copy-done.32, bf16[4,128,18]{1,2,0:T(8,128)(2,1)} %copy-done.31), kind=kOutput, calls=%fused_computation.110 | convolution fusion | flops 409681920 | bytes 2961920 | tf_op jit(solution)/shard_map/fh,xyhz->xyfz/dot_general | solution.py:134
  243.4 1.4 collective-permute-start.12
  244.8 1.7 collective-permute-start.13
  247.6 1.5 collective-permute-start.9
  249.5 5.0 collective-permute-done.9
  254.5 2.7 fusion.197
  257.3 2.0 all_gather.44
  260.2 31.6 %all-gather.10.cloned.1.call-done = bf16[32,80,2,128]{3,1,2,0:T(8,128)(2,1)} async-done(((bf16[8,80,2,128]{3,1,2,0:T(8,128)(2,1)}), bf16[32,80,2,128]{3,1,2,0:T(8,128)(2,1)}) %all-gather.10.cloned.1.call-update) | async-done | bytes 1310736 | tf_op jit(solution)/shard_map/all_gather | solution.py:161
  294.9 1.5 collective-permute-start.14
  296.4 7.3 %collective-permute-done.14 = bf16[16,40,2,128]{3,1,0,2:T(8,128)(2,1)S(1)} collective-permute-done((bf16[16,40,2,128]{3,1,0,2:T(8,128)(2,1)S(1)}, bf16[16,40,2,128]{3,1,0,2:T(8,128)(2,1)S(1)}, u32[]{:S(2)}, u32[]{:S(2)}) %collective-permute-start.14) | collective-permute-done | bytes 327712 | tf_op jit(solution)/shard_map/ppermute | solution.py:28
  305.1 1.5 collective-permute-start.15
  306.6 6.4 %collective-permute-done.15 = bf16[16,40,2,128]{3,1,0,2:T(8,128)(2,1)S(1)} collective-permute-done((bf16[16,40,2,128]{3,1,0,2:T(8,128)(2,1)S(1)}, bf16[16,40,2,128]{3,1,0,2:T(8,128)(2,1)S(1)}, u32[]{:S(2)}, u32[]{:S(2)}) %collective-permute-start.15) | collective-permute-done | bytes 327712 | tf_op jit(solution)/shard_map/ppermute | solution.py:28
  319.9 1.8 collective-permute-done.18
  325.4 24.1 %reduce-scatter.17.cloned.1.call-done = bf16[8,80,2,128]{3,1,2,0:T(8,128)(2,1)} async-done(((bf16[32,80,2,128]{3,1,2,0:T(8,128)(2,1)}), bf16[8,80,2,128]{3,1,2,0:T(8,128)(2,1)}) %reduce-scatter.17.cloned.1.call-update) | async-done | bytes 327696 | tf_op jit(solution)/shard_map/reduce_scatter | solution.py:144
  349.5 1.8 copy.209
  351.6 10.2 %convert_bitcast_fusion.1 = bf16[8,40,18,128]{3,2,1,0:T(8,128)(2,1)S(1)} fusion(f32[128]{0:T(128)S(1)} %get-tuple-element.74, bf16[8,40,18,128]{3,1,2,0:T(8,128)(2,1)} %bitcast.652, bf16[4,18,128]{2,1,0:T(8,128)(2,1)} %copy-done.32, bf16[4,128,18]{1,2,0:T(8,128)(2,1)} %copy-done.31), kind=kOutput, calls=%fused_computation.109 | convolution fusion | flops 409681920 | bytes 2961920 | tf_op jit(solution)/shard_map/fh,xyhz->xyfz/dot_general | solution.py:134
  361.9 1.4 collective-permute-start.19
  365.6 1.5 collective-permute-start.16
  367.6 5.0 collective-permute-done.16
  372.6 2.7 fusion.198
  375.3 2.0 all_gather.46
  378.2 31.6 %all-gather.12.cloned.1.call-done = bf16[32,80,2,128]{3,1,2,0:T(8,128)(2,1)} async-done(((bf16[8,80,2,128]{3,1,2,0:T(8,128)(2,1)}), bf16[32,80,2,128]{3,1,2,0:T(8,128)(2,1)}) %all-gather.12.cloned.1.call-update) | async-done | bytes 1310736 | tf_op jit(solution)/shard_map/all_gather | solution.py:161
  412.9 1.5 collective-permute-start.21
  414.4 7.3 %collective-permute-done.21 = bf16[16,40,2,128]{3,1,0,2:T(8,128)(2,1)S(1)} collective-permute-done((bf16[16,40,2,128]{3,1,0,2:T(8,128)(2,1)S(1)}, bf16[16,40,2,128]{3,1,0,2:T(8,128)(2,1)S(1)}, u32[]{:S(2)}, u32[]{:S(2)}) %collective-permute-start.21) | collective-permute-done | bytes 327712 | tf_op jit(solution)/shard_map/ppermute | solution.py:28
  423.1 1.5 collective-permute-start.22
  424.6 6.4 %collective-permute-done.22 = bf16[16,40,2,128]{3,1,0,2:T(8,128)(2,1)S(1)} collective-permute-done((bf16[16,40,2,128]{3,1,0,2:T(8,128)(2,1)S(1)}, bf16[16,40,2,128]{3,1,0,2:T(8,128)(2,1)S(1)}, u32[]{:S(2)}, u32[]{:S(2)}) %collective-permute-start.22) | collective-permute-done | bytes 327712 | tf_op jit(solution)/shard_map/ppermute | solution.py:28
  436.6 1.5 collective-permute-start.25
  438.1 1.5 collective-permute-done.25
  443.4 24.2 %reduce-scatter.21.cloned.1.call-done = bf16[8,80,2,128]{3,1,2,0:T(8,128)(2,1)} async-done(((bf16[32,80,2,128]{3,1,2,0:T(8,128)(2,1)}), bf16[8,80,2,128]{3,1,2,0:T(8,128)(2,1)}) %reduce-scatter.21.cloned.1.call-update) | async-done | bytes 327696 | tf_op jit(solution)/shard_map/reduce_scatter | solution.py:144
  467.5 1.8 copy.229
  469.4 10.2 %convert_bitcast_fusion = bf16[8,40,18,128]{3,2,1,0:T(8,128)(2,1)S(1)} fusion(f32[128]{0:T(128)S(1)} %get-tuple-element.76, bf16[8,40,18,128]{3,1,2,0:T(8,128)(2,1)} %bitcast.649, bf16[4,18,128]{2,1,0:T(8,128)(2,1)} %copy-done.32, bf16[4,128,18]{1,2,0:T(8,128)(2,1)} %copy-done.31), kind=kOutput, calls=%fused_computation.108 | convolution fusion | flops 409681920 | bytes 2961920 | tf_op jit(solution)/shard_map/fh,xyhz->xyfz/dot_general | solution.py:134
  479.6 1.3 collective-permute-start.26
  481.0 1.5 collective-permute-start.27
  483.6 1.5 collective-permute-start.23
  485.6 5.0 collective-permute-done.23
  490.6 2.7 fusion.240
  494.6 13.7 %all_to_all.12 = bf16[4,1,8,40,2,128]{5,4,3,2,1,0:T(2,128)(2,1)S(1)} all-to-all(bf16[4,1,8,40,2,128]{5,4,3,2,1,0:T(2,128)(2,1)S(1)} %maximum_bitcast_fusion), channel_id=1, replica_groups=mesh['section'=4,'coil'=4,'cuts'=2] {'section'}, dimensions={0} | all-to-all | bytes 1310720 | tf_op jit(solution)/shard_map/all_to_all | solution.py:255
  (316 shorter events, 77.2 us)
Async XLA Ops:
  6.5 38.8 %all-gather.14.cloned.1.call-start = ((), (), s32[]{:S(2)}) async-start(), calls=%async_computation.20 | async-start | bytes 1638400 | tf_op jit(solution)/shard_map/all_gather | solution.py:161
  10.1 101.5 %reduce-scatter.9.cloned.1.call-start = ((), (), s32[]{:S(2)}) async-start(), calls=%async_computation.9 | async-start | bytes 1638400 | tf_op jit(solution)/shard_map/reduce_scatter | solution.py:144
  12.2 35.2 %copy-start.11 = (bf16[128,128]{1,0:T(8,128)(2,1)}, bf16[128,128]{1,0:T(8,128)(2,1)S(1)}, u32[]{:S(2)}) copy-start(bf16[128,128]{1,0:T(8,128)(2,1)S(1)} %multiply_convert_fusion.2) | copy-start | bytes 98308
  12.5 34.9 %copy-start.15 = (bf16[128,128]{1,0:T(8,128)(2,1)}, bf16[128,128]{1,0:T(8,128)(2,1)S(1)}, u32[]{:S(2)}) copy-start(bf16[128,128]{1,0:T(8,128)(2,1)S(1)} %get-tuple-element.89) | copy-start | bytes 98308
  48.3 8.8 %collective-permute-start = (bf16[16,40,2,128]{3,1,0,2:T(8,128)(2,1)S(1)}, bf16[16,40,2,128]{3,1,0,2:T(8,128)(2,1)S(1)}, u32[]{:S(2)}, u32[]{:S(2)}) collective-permute-start(bf16[16,40,2,128]{3,1,0,2:T(8,128)(2,1)S(1)} %dynamic-slice_bitcast_fusion.8), channel_id=1, source_target_pairs={{0,8},{8,0},{16,24},{24,16},{1,9},{9,1},{17,25},{25,17},{2,10},{10... | collective-permute-start | bytes 983048 | tf_op jit(solution)/shard_map/ppermute | solution.py:28
  50.1 7.2 %copy-start.19 = (bf16[2,32,2,32,1]{1,3,0,4,2:T(8,128)(2,1)}, bf16[2,32,2,32,1]{1,3,0,4,2:T(8,128)(2,1)S(1)}, u32[]{:S(2)}) copy-start(bf16[2,32,2,32,1]{1,3,0,4,2:T(8,128)(2,1)S(1)} %copy.238) | copy-start | bytes 24580
  51.0 6.3 %copy-start.33 = (f32[40,128]{1,0:T(8,128)}, f32[40,128]{1,0:T(8,128)S(1)}, u32[]{:S(2)}) copy-start(f32[40,128]{1,0:T(8,128)S(1)} %convert_bitcast_fusion.4) | copy-start | bytes 61444
  58.4 8.0 %collective-permute-start.1 = (bf16[16,40,2,128]{3,1,0,2:T(8,128)(2,1)S(1)}, bf16[16,40,2,128]{3,1,0,2:T(8,128)(2,1)S(1)}, u32[]{:S(2)}, u32[]{:S(2)}) collective-permute-start(bf16[16,40,2,128]{3,1,0,2:T(8,128)(2,1)S(1)} %dynamic-slice_bitcast_fusion.7), channel_id=1, source_target_pairs={{0,8},{8,0},{16,24},{24,16},{1,9},{9,1},{17,25},{25,17},{2,10},{10... | collective-permute-start | bytes 983048 | tf_op jit(solution)/shard_map/ppermute | solution.py:28
  60.5 7.0 %copy-start.23 = (bf16[128,128]{1,0:T(8,128)(2,1)}, bf16[128,128]{1,0:T(8,128)(2,1)S(1)}, u32[]{:S(2)}) copy-start(bf16[128,128]{1,0:T(8,128)(2,1)S(1)} %get-tuple-element.91) | copy-start | bytes 98308
  60.5 7.0 %copy-start.27 = (bf16[128,128]{1,0:T(8,128)(2,1)}, bf16[128,128]{1,0:T(8,128)(2,1)S(1)}, u32[]{:S(2)}) copy-start(bf16[128,128]{1,0:T(8,128)(2,1)S(1)} %get-tuple-element.92) | copy-start | bytes 98308
  70.6 12.7 %copy-start.37 = (bf16[1,128,18]{1,2,0:T(8,128)(2,1)S(1)}, bf16[1,128,18]{1,2,0:T(8,128)(2,1)}, u32[]{:S(2)}) copy-start(bf16[1,128,18]{1,2,0:T(8,128)(2,1)} %param.13) | copy-start | bytes 13828
  70.6 29.8 %copy-start.38 = (bf16[1,18,128]{2,1,0:T(8,128)(2,1)S(1)}, bf16[1,18,128]{2,1,0:T(8,128)(2,1)}, u32[]{:S(2)}) copy-start(bf16[1,18,128]{2,1,0:T(8,128)(2,1)} %param.15) | copy-start | bytes 13828
  70.7 56.7 %reduce-scatter.11.cloned.1.call-start = ((), (), s32[]{:S(2)}) async-start(), calls=%async_computation.10 | async-start | bytes 491520 | tf_op jit(solution)/shard_map/reduce_scatter | solution.py:150
  70.9 37.0 %collective-permute-start.3 = (bf16[8,1,2,128]{3,2,1,0:T(2,128)(2,1)S(1)}, bf16[8,1,2,128]{3,2,1,0:T(2,128)(2,1)S(1)}, u32[]{:S(2)}, u32[]{:S(2)}) collective-permute-start(bf16[8,1,2,128]{3,2,1,0:T(2,128)(2,1)S(1)} %get-tuple-element.67), channel_id=1, source_target_pairs={{0,1},{2,3},{4,5},{6,7},{8,9},{10,11},{12,13},{14,15},{16,17},{18,... | collective-permute-start | bytes 12296 | tf_op jit(solution)/shard_map/ppermute | solution.py:15
  72.2 35.7 %collective-permute-start.4 = (bf16[8,1,2,128]{3,2,1,0:T(2,128)(2,1)S(1)}, bf16[8,1,2,128]{3,2,1,0:T(2,128)(2,1)S(1)}, u32[]{:S(2)}, u32[]{:S(2)}) collective-permute-start(bf16[8,1,2,128]{3,2,1,0:T(2,128)(2,1)S(1)} %get-tuple-element.68), channel_id=1, source_target_pairs={{1,0},{3,2},{5,4},{7,6},{9,8},{11,10},{13,12},{15,14},{17,16},{19,... | collective-permute-start | bytes 12296 | tf_op jit(solution)/shard_map/ppermute | solution.py:16
  91.5 22.0 %copy-start.31 = (bf16[4,128,18]{1,2,0:T(8,128)(2,1)}, bf16[4,128,18]{1,2,0:T(8,128)(2,1)S(1)}, u32[]{:S(2)}) copy-start(bf16[4,128,18]{1,2,0:T(8,128)(2,1)S(1)} %all_gather.39) | copy-start | bytes 55300
  107.9 5.6 %copy-start.32 = (bf16[4,18,128]{2,1,0:T(8,128)(2,1)}, bf16[4,18,128]{2,1,0:T(8,128)(2,1)S(1)}, u32[]{:S(2)}) copy-start(bf16[4,18,128]{2,1,0:T(8,128)(2,1)S(1)} %all_gather.41) | copy-start | bytes 55300
  113.4 60.1 %all-gather.8.cloned.1.call-start = ((), (), s32[]{:S(2)}) async-start(), calls=%async_computation.11 | async-start | bytes 1638400 | tf_op jit(solution)/shard_map/all_gather | solution.py:161
  123.8 6.2 %collective-permute-start.5 = (bf16[8,1,18,128]{3,2,1,0:T(8,128)(2,1)S(1)}, bf16[8,1,18,128]{3,2,1,0:T(8,128)(2,1)S(1)}, u32[]{:S(2)}, u32[]{:S(2)}) collective-permute-start(bf16[8,1,18,128]{3,2,1,0:T(8,128)(2,1)S(1)} %get-tuple-element.25), channel_id=1, source_target_pairs={{0,1},{2,3},{4,5},{6,7},{8,9},{10,11},{12,13},{14,15},{16,17},{18,... | collective-permute-start | bytes 110600 | tf_op jit(solution)/shard_map/ppermute | solution.py:15
  125.1 4.9 collective-permute-start.6
  128.5 7.0 %copy-start.3 = (bf16[8,40,2,128]{3,0,2,1:T(8,128)(2,1)S(1)}, bf16[8,40,2,128]{3,0,2,1:T(8,128)(2,1)}, u32[]{:S(2)}) copy-start(bf16[8,40,2,128]{3,0,2,1:T(8,128)(2,1)} %reduce-scatter.11.cloned.1.call-done) | copy-start | bytes 491524
  128.5 7.0 %collective-permute-start.2 = (bf16[8,40,2,128]{3,2,1,0:T(2,128)(2,1)S(1)}, bf16[8,40,2,128]{3,2,1,0:T(2,128)(2,1)S(1)}, u32[]{:S(2)}, u32[]{:S(2)}) collective-permute-start(bf16[8,40,2,128]{3,2,1,0:T(2,128)(2,1)S(1)} %copy.169), channel_id=1, source_target_pairs={{0,8},{8,0},{16,24},{24,16},{1,9},{9,1},{17,25},{25,17},{2,10},{10... | collective-permute-start | bytes 491528 | tf_op jit(solution)/shard_map/ppermute | solution.py:28
  141.1 90.2 %reduce-scatter.13.cloned.1.call-start = ((), (), s32[]{:S(2)}) async-start(), calls=%async_computation.12 | async-start | bytes 1638400 | tf_op jit(solution)/shard_map/reduce_scatter | solution.py:144
  176.6 9.0 %copy-start.8 = (bf16[1,1,32,40,2,128]{5,4,3,2,1,0:T(2,128)(2,1)S(1)}, bf16[1,1,32,40,2,128]{5,4,3,2,1,0:T(2,128)(2,1)}, u32[]{:S(2)}) copy-start(bf16[1,1,32,40,2,128]{5,4,3,2,1,0:T(2,128)(2,1)} %copy-done.7) | copy-start | bytes 1966084
  176.6 9.0 %copy-start.20 = (bf16[2,32,2,32,1]{1,3,0,4,2:T(8,128)(2,1)S(1)}, bf16[2,32,2,32,1]{1,3,0,4,2:T(8,128)(2,1)}, u32[]{:S(2)}) copy-start(bf16[2,32,2,32,1]{1,3,0,4,2:T(8,128)(2,1)} %copy-done.19) | copy-start | bytes 24580
  176.6 9.0 %copy-start.34 = (f32[40,128]{1,0:T(8,128)S(1)}, f32[40,128]{1,0:T(8,128)}, u32[]{:S(2)}) copy-start(f32[40,128]{1,0:T(8,128)} %copy-done.33) | copy-start | bytes 61444
  176.6 8.8 %collective-permute-start.7 = (bf16[16,40,2,128]{3,1,0,2:T(8,128)(2,1)S(1)}, bf16[16,40,2,128]{3,1,0,2:T(8,128)(2,1)S(1)}, u32[]{:S(2)}, u32[]{:S(2)}) collective-permute-start(bf16[16,40,2,128]{3,1,0,2:T(8,128)(2,1)S(1)} %dynamic-slice_bitcast_fusion.6), channel_id=1, source_target_pairs={{0,8},{8,0},{16,24},{24,16},{1,9},{9,1},{17,25},{25,17},{2,10},{10... | collective-permute-start | bytes 983048 | tf_op jit(solution)/shard_map/ppermute | solution.py:28
  186.8 7.9 %collective-permute-start.8 = (bf16[16,40,2,128]{3,1,0,2:T(8,128)(2,1)S(1)}, bf16[16,40,2,128]{3,1,0,2:T(8,128)(2,1)S(1)}, u32[]{:S(2)}, u32[]{:S(2)}) collective-permute-start(bf16[16,40,2,128]{3,1,0,2:T(8,128)(2,1)S(1)} %dynamic-slice_bitcast_fusion.5), channel_id=1, source_target_pairs={{0,8},{8,0},{16,24},{24,16},{1,9},{9,1},{17,25},{25,17},{2,10},{10... | collective-permute-start | bytes 983048 | tf_op jit(solution)/shard_map/ppermute | solution.py:28
  199.0 47.5 %reduce-scatter.15.cloned.1.call-start = ((), (), s32[]{:S(2)}) async-start(), calls=%async_computation.13 | async-start | bytes 491520 | tf_op jit(solution)/shard_map/reduce_scatter | solution.py:150
  199.0 2.8 collective-permute-start.10
  200.3 3.1 collective-permute-start.11
  233.1 58.7 %all-gather.10.cloned.1.call-start = ((), (), s32[]{:S(2)}) async-start(), calls=%async_computation.14 | async-start | bytes 1638400 | tf_op jit(solution)/shard_map/all_gather | solution.py:161
  243.4 5.7 %collective-permute-start.12 = (bf16[8,1,18,128]{3,2,1,0:T(8,128)(2,1)S(1)}, bf16[8,1,18,128]{3,2,1,0:T(8,128)(2,1)S(1)}, u32[]{:S(2)}, u32[]{:S(2)}) collective-permute-start(bf16[8,1,18,128]{3,2,1,0:T(8,128)(2,1)S(1)} %get-tuple-element.21), channel_id=1, source_target_pairs={{0,1},{2,3},{4,5},{6,7},{8,9},{10,11},{12,13},{14,15},{16,17},{18,... | collective-permute-start | bytes 110600 | tf_op jit(solution)/shard_map/ppermute | solution.py:15
  244.8 4.3 collective-permute-start.13
  247.6 7.0 %copy-start.5 = (bf16[8,40,2,128]{3,0,2,1:T(8,128)(2,1)S(1)}, bf16[8,40,2,128]{3,0,2,1:T(8,128)(2,1)}, u32[]{:S(2)}) copy-start(bf16[8,40,2,128]{3,0,2,1:T(8,128)(2,1)} %reduce-scatter.15.cloned.1.call-done) | copy-start | bytes 491524
  247.6 7.0 %collective-permute-start.9 = (bf16[8,40,2,128]{3,2,1,0:T(2,128)(2,1)S(1)}, bf16[8,40,2,128]{3,2,1,0:T(2,128)(2,1)S(1)}, u32[]{:S(2)}, u32[]{:S(2)}) collective-permute-start(bf16[8,40,2,128]{3,2,1,0:T(2,128)(2,1)S(1)} %copy.190), channel_id=1, source_target_pairs={{0,8},{8,0},{16,24},{24,16},{1,9},{9,1},{17,25},{25,17},{2,10},{10... | collective-permute-start | bytes 491528 | tf_op jit(solution)/shard_map/ppermute | solution.py:28
  260.1 89.4 %reduce-scatter.17.cloned.1.call-start = ((), (), s32[]{:S(2)}) async-start(), calls=%async_computation.15 | async-start | bytes 1638400 | tf_op jit(solution)/shard_map/reduce_scatter | solution.py:144
  294.8 9.1 %copy-start.9 = (bf16[1,1,32,40,2,128]{5,4,3,2,1,0:T(2,128)(2,1)S(1)}, bf16[1,1,32,40,2,128]{5,4,3,2,1,0:T(2,128)(2,1)}, u32[]{:S(2)}) copy-start(bf16[1,1,32,40,2,128]{5,4,3,2,1,0:T(2,128)(2,1)} %copy-done.7) | copy-start | bytes 1966084
  294.8 9.1 %copy-start.21 = (bf16[2,32,2,32,1]{1,3,0,4,2:T(8,128)(2,1)S(1)}, bf16[2,32,2,32,1]{1,3,0,4,2:T(8,128)(2,1)}, u32[]{:S(2)}) copy-start(bf16[2,32,2,32,1]{1,3,0,4,2:T(8,128)(2,1)} %copy-done.19) | copy-start | bytes 24580
  294.9 9.1 %copy-start.35 = (f32[40,128]{1,0:T(8,128)S(1)}, f32[40,128]{1,0:T(8,128)}, u32[]{:S(2)}) copy-start(f32[40,128]{1,0:T(8,128)} %copy-done.33) | copy-start | bytes 61444
  294.9 8.8 %collective-permute-start.14 = (bf16[16,40,2,128]{3,1,0,2:T(8,128)(2,1)S(1)}, bf16[16,40,2,128]{3,1,0,2:T(8,128)(2,1)S(1)}, u32[]{:S(2)}, u32[]{:S(2)}) collective-permute-start(bf16[16,40,2,128]{3,1,0,2:T(8,128)(2,1)S(1)} %dynamic-slice_bitcast_fusion.4), channel_id=1, source_target_pairs={{0,8},{8,0},{16,24},{24,16},{1,9},{9,1},{17,25},{25,17},{2,10},{10... | collective-permute-start | bytes 983048 | tf_op jit(solution)/shard_map/ppermute | solution.py:28
  305.1 8.0 %collective-permute-start.15 = (bf16[16,40,2,128]{3,1,0,2:T(8,128)(2,1)S(1)}, bf16[16,40,2,128]{3,1,0,2:T(8,128)(2,1)S(1)}, u32[]{:S(2)}, u32[]{:S(2)}) collective-permute-start(bf16[16,40,2,128]{3,1,0,2:T(8,128)(2,1)S(1)} %dynamic-slice_bitcast_fusion.3), channel_id=1, source_target_pairs={{0,8},{8,0},{16,24},{24,16},{1,9},{9,1},{17,25},{25,17},{2,10},{10... | collective-permute-start | bytes 983048 | tf_op jit(solution)/shard_map/ppermute | solution.py:28
  317.3 47.3 %reduce-scatter.19.cloned.1.call-start = ((), (), s32[]{:S(2)}) async-start(), calls=%async_computation.16 | async-start | bytes 491520 | tf_op jit(solution)/shard_map/reduce_scatter | solution.py:150
  317.3 2.6 collective-permute-start.17
  318.6 3.1 collective-permute-start.18
  351.4 58.5 %all-gather.12.cloned.1.call-start = ((), (), s32[]{:S(2)}) async-start(), calls=%async_computation.17 | async-start | bytes 1638400 | tf_op jit(solution)/shard_map/all_gather | solution.py:161
  361.9 5.3 %collective-permute-start.19 = (bf16[8,1,18,128]{3,2,1,0:T(8,128)(2,1)S(1)}, bf16[8,1,18,128]{3,2,1,0:T(8,128)(2,1)S(1)}, u32[]{:S(2)}, u32[]{:S(2)}) collective-permute-start(bf16[8,1,18,128]{3,2,1,0:T(8,128)(2,1)S(1)} %get-tuple-element.15), channel_id=1, source_target_pairs={{0,1},{2,3},{4,5},{6,7},{8,9},{10,11},{12,13},{14,15},{16,17},{18,... | collective-permute-start | bytes 110600 | tf_op jit(solution)/shard_map/ppermute | solution.py:15
  363.2 3.9 collective-permute-start.20
  365.6 7.0 %copy-start.6 = (bf16[8,40,2,128]{3,0,2,1:T(8,128)(2,1)S(1)}, bf16[8,40,2,128]{3,0,2,1:T(8,128)(2,1)}, u32[]{:S(2)}) copy-start(bf16[8,40,2,128]{3,0,2,1:T(8,128)(2,1)} %reduce-scatter.19.cloned.1.call-done) | copy-start | bytes 491524
  365.6 7.0 %collective-permute-start.16 = (bf16[8,40,2,128]{3,2,1,0:T(2,128)(2,1)S(1)}, bf16[8,40,2,128]{3,2,1,0:T(2,128)(2,1)S(1)}, u32[]{:S(2)}, u32[]{:S(2)}) collective-permute-start(bf16[8,40,2,128]{3,2,1,0:T(2,128)(2,1)S(1)} %copy.210), channel_id=1, source_target_pairs={{0,8},{8,0},{16,24},{24,16},{1,9},{9,1},{17,25},{25,17},{2,10},{10... | collective-permute-start | bytes 491528 | tf_op jit(solution)/shard_map/ppermute | solution.py:28
  378.1 89.4 %reduce-scatter.21.cloned.1.call-start = ((), (), s32[]{:S(2)}) async-start(), calls=%async_computation.18 | async-start | bytes 1638400 | tf_op jit(solution)/shard_map/reduce_scatter | solution.py:144
  412.9 9.0 %copy-start.10 = (bf16[1,1,32,40,2,128]{5,4,3,2,1,0:T(2,128)(2,1)S(1)}, bf16[1,1,32,40,2,128]{5,4,3,2,1,0:T(2,128)(2,1)}, u32[]{:S(2)}) copy-start(bf16[1,1,32,40,2,128]{5,4,3,2,1,0:T(2,128)(2,1)} %copy-done.7) | copy-start | bytes 1966084
  412.9 9.0 %copy-start.22 = (bf16[2,32,2,32,1]{1,3,0,4,2:T(8,128)(2,1)S(1)}, bf16[2,32,2,32,1]{1,3,0,4,2:T(8,128)(2,1)}, u32[]{:S(2)}) copy-start(bf16[2,32,2,32,1]{1,3,0,4,2:T(8,128)(2,1)} %copy-done.19) | copy-start | bytes 24580
  412.9 9.0 %copy-start.36 = (f32[40,128]{1,0:T(8,128)S(1)}, f32[40,128]{1,0:T(8,128)}, u32[]{:S(2)}) copy-start(f32[40,128]{1,0:T(8,128)} %copy-done.33) | copy-start | bytes 61444
  412.9 8.8 %collective-permute-start.21 = (bf16[16,40,2,128]{3,1,0,2:T(8,128)(2,1)S(1)}, bf16[16,40,2,128]{3,1,0,2:T(8,128)(2,1)S(1)}, u32[]{:S(2)}, u32[]{:S(2)}) collective-permute-start(bf16[16,40,2,128]{3,1,0,2:T(8,128)(2,1)S(1)} %dynamic-slice_bitcast_fusion.2), channel_id=1, source_target_pairs={{0,8},{8,0},{16,24},{24,16},{1,9},{9,1},{17,25},{25,17},{2,10},{10... | collective-permute-start | bytes 983048 | tf_op jit(solution)/shard_map/ppermute | solution.py:28
  423.1 7.9 %collective-permute-start.22 = (bf16[16,40,2,128]{3,1,0,2:T(8,128)(2,1)S(1)}, bf16[16,40,2,128]{3,1,0,2:T(8,128)(2,1)S(1)}, u32[]{:S(2)}, u32[]{:S(2)}) collective-permute-start(bf16[16,40,2,128]{3,1,0,2:T(8,128)(2,1)S(1)} %dynamic-slice_bitcast_fusion.1), channel_id=1, source_target_pairs={{0,8},{8,0},{16,24},{24,16},{1,9},{9,1},{17,25},{25,17},{2,10},{10... | collective-permute-start | bytes 983048 | tf_op jit(solution)/shard_map/ppermute | solution.py:28
  435.3 47.3 %reduce-scatter.23.cloned.1.call-start = ((), (), s32[]{:S(2)}) async-start(), calls=%async_computation.19 | async-start | bytes 491520 | tf_op jit(solution)/shard_map/reduce_scatter | solution.py:150
  435.3 2.8 collective-permute-start.24
  436.6 3.1 collective-permute-start.25
  479.6 5.5 %collective-permute-start.26 = (bf16[8,1,18,128]{3,2,1,0:T(8,128)(2,1)S(1)}, bf16[8,1,18,128]{3,2,1,0:T(8,128)(2,1)S(1)}, u32[]{:S(2)}, u32[]{:S(2)}) collective-permute-start(bf16[8,1,18,128]{3,2,1,0:T(8,128)(2,1)S(1)} %get-tuple-element.9), channel_id=1, source_target_pairs={{0,1},{2,3},{4,5},{6,7},{8,9},{10,11},{12,13},{14,15},{16,17},{18,... | collective-permute-start | bytes 110600 | tf_op jit(solution)/shard_map/ppermute | solution.py:15
  481.0 4.2 collective-permute-start.27
  483.6 7.0 %copy-start.4 = (bf16[8,40,2,128]{3,0,2,1:T(8,128)(2,1)S(1)}, bf16[8,40,2,128]{3,0,2,1:T(8,128)(2,1)}, u32[]{:S(2)}) copy-start(bf16[8,40,2,128]{3,0,2,1:T(8,128)(2,1)} %reduce-scatter.23.cloned.1.call-done) | copy-start | bytes 491524
  483.6 7.0 %collective-permute-start.23 = (bf16[8,40,2,128]{3,2,1,0:T(2,128)(2,1)S(1)}, bf16[8,40,2,128]{3,2,1,0:T(2,128)(2,1)S(1)}, u32[]{:S(2)}, u32[]{:S(2)}) collective-permute-start(bf16[8,40,2,128]{3,2,1,0:T(2,128)(2,1)S(1)} %copy.230), channel_id=1, source_target_pairs={{0,8},{8,0},{16,24},{24,16},{1,9},{9,1},{17,25},{25,17},{2,10},{10... | collective-permute-start | bytes 491528 | tf_op jit(solution)/shard_map/ppermute | solution.py:28
  493.3 15.8 %copy-start.1 = (bf16[2,1,32,80,2,128]{5,4,3,2,1,0:T(2,128)(2,1)S(1)}, bf16[2,1,32,80,2,128]{5,4,3,2,1,0:T(2,128)(2,1)}, u32[]{:S(2)}) copy-start(bf16[2,1,32,80,2,128]{5,4,3,2,1,0:T(2,128)(2,1)} %param.9) | copy-start | bytes 7864324
  (17 other events, 30.4 us)
Sparse Core Ops, SparseCore 0:
  10.2 35.1 all-gather.13
  70.8 32.0 reduce-scatter.8
  113.6 7.5 reduce-scatter.10
  141.2 32.3 all-gather.7
  199.1 32.1 reduce-scatter.12
  233.3 6.4 reduce-scatter.14
  260.2 31.5 all-gather.9
  317.4 32.0 reduce-scatter.16
  351.8 6.4 reduce-scatter.18
  378.3 31.5 all-gather.11
  435.4 32.1 reduce-scatter.20
  469.6 6.4 reduce-scatter.22
where the time goes:
time: 525 us; the launch traced here: 516 us
  waiting for transfers between devices  278 us (53%)
  blocking collectives  54.4 us (10%)
  matrix products  49.7 us (9%)
  local copies, waits for them, and re-layouts  44.4 us (8%)
  starting transfers between devices  41.4 us (8%)
  other arithmetic  32.6 us (6%)
  between operations  16.4 us (3%)
    all_gather x4, waiting for transfers between devices, pair_block(): whole = lax.all_gather(halves, 'coil', axis=0, tiled=True)  129 us
    reduce_scatter x4, waiting for transfers between devices, sum_gradient(): lax.psum_scatter(back_rows(jnp.int32(0), lax.axis_size('coil') * current....  72.5 us
    ppermute x12, waiting for transfers between devices, from_partner(): return lax.ppermute(block, axis, route)  71.4 us
    dot_general x4, matrix products, refine_rows(): jnp.einsum('fh,xyhz->xyfz', weights_out, hidden, preferred_element_type=j...  40.9 us
    ppermute x12, starting transfers between devices, from_partner(): return lax.ppermute(block, axis, route)  18.4 us
    all_to_all x1, blocking collectives, body(): lax.all_to_all(stacked, 'section', split_axis=0, concat_axis=1, tiled=True)  13.7 us
    ppermute x8, starting transfers between devices, extended_2(): after = lax.ppermute(leading, axis, down)  11.8 us
    ppermute x8, starting transfers between devices, extended_2(): before = lax.ppermute(last, axis, up)  10.5 us
  transfers between devices with their start and end apart: 40, of which 22 were waited for; matrix products, arithmetic and copies ran while one was open for 13% of the time, Pallas kernels for 0%

commit v1 on v0

--- a/solution.py
+++ b/solution.py
@@ -3,6 +3,17 @@
 import jax.numpy as jnp
 from jax import lax
 from jax.sharding import PartitionSpec as P
+
+
+def pass_along(shard, axis, d):
+    size = lax.axis_size(axis)
+    right = [(i, (i + 1) % size) for i in range(size)]
+    shards = [shard]
+    for hop in range(1, size):
+        shards = [lax.ppermute(shards[0], axis, right), *shards]
+    whole = jnp.concatenate(shards, axis=d)
+    turn = (lax.axis_index(axis) + 1) * shards[-1].shape[d]
+    return jnp.roll(whole, turn, axis=d)
 
 
 def extended_2(x, sides, width):
@@ -158,7 +169,7 @@
 
 def pair_block(current, sens_one, data_one, mask_one, step, weights_in, bias, weights_out, half):
     halves = whole_rows(current)
-    whole = lax.all_gather(halves, "coil", axis=0, tiled=True)
+    whole = pass_along(halves, "coil", 0)
     size_x, size_y, _, size_z = whole.shape
     half_x = size_x // 2
     half_y = size_y // 2

time: 525 us -> 510 us (0.971)
  waiting for transfers between devices: 278 us -> 258 us
  other arithmetic: 32.6 us -> 25.7 us
    all_gather x4 -> x0, waiting for transfers between devices: 129 us -> none  [pair_block(): whole = lax.all_gather(halves, 'coil', axis=0, tiled=True)]
    ppermute x0 -> x12, waiting for transfers between devices: none -> 126 us  [pass_along(): shards = [lax.ppermute(shards[0], axis, right), *shards]]
    ppermute x12, waiting for transfers between devices: 71.4 us -> 59.9 us  [from_partner(): return lax.ppermute(block, axis, route)]
    dot_general x0 -> x4, local copies, waits for them, and re-layouts: none -> 6.95 us  [refine_rows(): jnp.einsum('fh,xyhz->xyfz', weights_out, hidden, preferred_element_type=j...]
    reduce_scatter x4, waiting for transfers between devices: 72.5 us -> 66.9 us  [sum_gradient(): lax.psum_scatter(back_rows(jnp.int32(0), lax.axis_size('coil') * current....]
  transfers between devices with their start and end apart: 40 -> 48, of which waited for: 22 -> 30; matrix products, arithmetic and copies ran while one was open for 13% -> 16% of each run, Pallas kernels for 0% -> 0%
where the time goes in v1:
time: 510 us; the launch traced here: 500 us
  waiting for transfers between devices  258 us (51%)
  blocking collectives  54.8 us (11%)
  matrix products  53.9 us (11%)
  local copies, waits for them, and re-layouts  46.6 us (9%)
  starting transfers between devices  45 us (9%)
  other arithmetic  25.7 us (5%)
  between operations  16.3 us (3%)
    ppermute x12, waiting for transfers between devices, pass_along(): shards = [lax.ppermute(shards[0], axis, right), *shards]  126 us
    reduce_scatter x4, waiting for transfers between devices, sum_gradient(): lax.psum_scatter(back_rows(jnp.int32(0), lax.axis_size('coil') * current....  66.9 us
    ppermute x12, waiting for transfers between devices, from_partner(): return lax.ppermute(block, axis, route)  59.9 us
    dot_general x4, matrix products, refine_rows(): jnp.einsum('fh,xyhz->xyfz', weights_out, hidden, preferred_element_type=j...  45.2 us
    ppermute x12, starting transfers between devices, from_partner(): return lax.ppermute(block, axis, route)  19.3 us
    all_to_all x1, blocking collectives, body(): lax.all_to_all(stacked, 'section', split_axis=0, concat_axis=1, tiled=True)  13.8 us
    ppermute x8, starting transfers between devices, extended_2(): after = lax.ppermute(leading, axis, down)  10.6 us
    ppermute x8, starting transfers between devices, extended_2(): before = lax.ppermute(last, axis, up)  10.5 us
  transfers between devices with their start and end apart: 48, of which 30 were waited for; matrix products, arithmetic and copies ran while one was open for 16% of the time, Pallas kernels for 0%

profile of v1, /device:TPU:0, one launch (start us, length us, event | category | flops | bytes accessed | tf_op | source)
XLA Modules:
  0.0 500.0 jit_solution(15647424689351653370)
XLA Ops:
  7.8 2.2 all-gather
  9.9 2.9 collective-permute-start
  13.8 9.2 %collective-permute-done = bf16[8,80,2,128]{3,1,2,0:T(8,128)(2,1)} collective-permute-done((bf16[8,80,2,128]{3,1,2,0:T(8,128)(2,1)S(1)}, bf16[8,80,2,128]{3,1,2,0:T(8,128)(2,1)}, u32[]{:S(2)}, u32[]{:S(2)}) %collective-permute-start) | collective-permute-done | bytes 327712 | tf_op jit(solution)/shard_map/ppermute | solution.py:13
  23.7 10.5 %collective-permute-done.1 = bf16[8,80,2,128]{3,1,2,0:T(8,128)(2,1)} collective-permute-done((bf16[8,80,2,128]{3,1,2,0:T(8,128)(2,1)}, bf16[8,80,2,128]{3,1,2,0:T(8,128)(2,1)}, u32[]{:S(2)}, u32[]{:S(2)}) %collective-permute-start.1) | collective-permute-done | bytes 327712 | tf_op jit(solution)/shard_map/ppermute | solution.py:13
  34.9 9.7 %collective-permute-done.2 = bf16[8,80,2,128]{3,1,2,0:T(8,128)(2,1)S(1)} collective-permute-done((bf16[8,80,2,128]{3,1,2,0:T(8,128)(2,1)}, bf16[8,80,2,128]{3,1,2,0:T(8,128)(2,1)S(1)}, u32[]{:S(2)}, u32[]{:S(2)}) %collective-permute-start.2) | collective-permute-done | bytes 327712 | tf_op jit(solution)/shard_map/ppermute | solution.py:13
  47.4 2.2 collective-permute-start.3
  50.8 1.6 constant_dynamic-slice_fusion
  52.3 2.7 collective-permute-done.3
  56.4 1.8 collective-permute-start.4
  58.8 4.8 collective-permute-done.4
  72.6 8.2 %all-gather.1 = f32[4,1,128]{2,1,0:T(1,128)S(1)} all-gather(f32[1,1,128]{2,1,0:T(1,128)S(1)} %bitcast.672), channel_id=1, replica_groups=mesh['section'=4,'coil'=4,'cuts'=2] {'section'}, dimensions={0}, use_global_device_ids=true | all-gather | bytes 2560 | tf_op jit(solution)/shard_map/all_gather | solution.py:239
  81.3 8.2 %all_gather.26 = bf16[4,128,18]{1,2,0:T(8,128)(2,1)S(1)} all-gather(bf16[1,128,18]{1,2,0:T(8,128)(2,1)S(1)} %copy-done.29), channel_id=1, replica_groups=mesh['section'=4,'coil'=4,'cuts'=2] {'section'}, dimensions={0}, use_global_device_ids=true | all-gather | bytes 23040 | tf_op jit(solution)/shard_map/all_gather | solution.py:242
  89.5 8.9 %all-reduce.8 = f32[4]{0:T(128)S(1)} all-reduce(f32[4]{0:T(128)S(1)} %dynamic-update-slice), channel_id=1, replica_groups=mesh['section'=4,'coil'=4,'cuts'=2] {'section'}, use_global_device_ids=true, to_apply=%add.8 | all-reduce | flops 4 | bytes 32
  98.4 7.4 %all_gather.28 = bf16[4,18,128]{2,1,0:T(8,128)(2,1)S(1)} all-gather(bf16[1,18,128]{2,1,0:T(8,128)(2,1)S(1)} %copy-done.30), channel_id=1, replica_groups=mesh['section'=4,'coil'=4,'cuts'=2] {'section'}, dimensions={0}, use_global_device_ids=true | all-gather | bytes 23040 | tf_op jit(solution)/shard_map/all_gather | solution.py:243
  108.5 1.8 copy.298
  110.4 11.3 %fusion.22 = bf16[8,40,128,18]{2,3,1,0:T(8,128)(2,1)} fusion(f32[128]{0:T(128)S(1)} %get-tuple-element.76, bf16[8,40,18,128]{3,1,2,0:T(8,128)(2,1)} %bitcast.655, bf16[4,18,128]{2,1,0:T(8,128)(2,1)S(1)} %all_gather.28, bf16[4,128,18]{1,2,0:T(8,128)(2,1)S(1)} %all_gather.26), kind=kOutput, calls=%fused_computation.51 | convolution fusion | flops 408944640 | bytes 2961920 | tf_op jit(solution)/shard_map/fh,xyhz->xyfz/dot_general | solution.py:145
  121.7 1.7 copy.622
  127.8 1.5 collective-permute-start.5
  130.2 4.6 collective-permute-done.5
  136.0 2.0 all_gather.29
  138.0 11.6 %collective-permute-done.10 = bf16[8,80,2,128]{3,1,2,0:T(8,128)(2,1)S(1)} collective-permute-done((bf16[8,80,2,128]{3,1,2,0:T(8,128)(2,1)S(1)}, bf16[8,80,2,128]{3,1,2,0:T(8,128)(2,1)S(1)}, u32[]{:S(2)}, u32[]{:S(2)}) %collective-permute-start.10) | collective-permute-done | bytes 327712 | tf_op jit(solution)/shard_map/ppermute | solution.py:13
  149.6 10.7 %collective-permute-done.11 = bf16[8,80,2,128]{3,1,2,0:T(8,128)(2,1)S(1)} collective-permute-done((bf16[8,80,2,128]{3,1,2,0:T(8,128)(2,1)S(1)}, bf16[8,80,2,128]{3,1,2,0:T(8,128)(2,1)S(1)}, u32[]{:S(2)}, u32[]{:S(2)}) %collective-permute-start.11) | collective-permute-done | bytes 327712 | tf_op jit(solution)/shard_map/ppermute | solution.py:13
  160.5 9.8 %collective-permute-done.12 = bf16[8,80,2,128]{3,1,2,0:T(8,128)(2,1)S(1)} collective-permute-done((bf16[8,80,2,128]{3,1,2,0:T(8,128)(2,1)S(1)}, bf16[8,80,2,128]{3,1,2,0:T(8,128)(2,1)S(1)}, u32[]{:S(2)}, u32[]{:S(2)}) %collective-permute-start.12) | collective-permute-done | bytes 327712 | tf_op jit(solution)/shard_map/ppermute | solution.py:13
  173.3 1.5 collective-permute-start.13
  174.8 5.7 %collective-permute-done.13 = bf16[16,40,2,128]{3,1,0,2:T(8,128)(2,1)S(1)} collective-permute-done((bf16[16,40,2,128]{3,1,0,2:T(8,128)(2,1)S(1)}, bf16[16,40,2,128]{3,1,0,2:T(8,128)(2,1)S(1)}, u32[]{:S(2)}, u32[]{:S(2)}) %collective-permute-start.13) | collective-permute-done | bytes 327712 | tf_op jit(solution)/shard_map/ppermute | solution.py:39
  181.9 1.5 collective-permute-start.14
  183.4 5.6 %collective-permute-done.14 = bf16[16,40,2,128]{3,1,0,2:T(8,128)(2,1)S(1)} collective-permute-done((bf16[16,40,2,128]{3,1,0,2:T(8,128)(2,1)S(1)}, bf16[16,40,2,128]{3,1,0,2:T(8,128)(2,1)S(1)}, u32[]{:S(2)}, u32[]{:S(2)}) %collective-permute-start.14) | collective-permute-done | bytes 327712 | tf_op jit(solution)/shard_map/ppermute | solution.py:39
  196.0 1.8 collective-permute-done.17
  200.4 21.7 %reduce-scatter.13.cloned.1.call-done = bf16[8,80,2,128]{3,1,2,0:T(8,128)(2,1)} async-done(((bf16[32,80,2,128]{3,1,2,0:T(8,128)(2,1)}), bf16[8,80,2,128]{3,1,2,0:T(8,128)(2,1)}) %reduce-scatter.13.cloned.1.call-update) | async-done | bytes 327696 | tf_op jit(solution)/shard_map/reduce_scatter | solution.py:155
  222.1 1.8 copy.318
  224.4 11.3 %fusion.20 = bf16[8,40,128,18]{2,3,1,0:T(8,128)(2,1)} fusion(f32[128]{0:T(128)S(1)} %copy-done.33, bf16[8,40,18,128]{3,1,2,0:T(8,128)(2,1)} %bitcast.656, bf16[4,18,128]{2,1,0:T(8,128)(2,1)} %copy-done.24, bf16[4,128,18]{1,2,0:T(8,128)(2,1)S(1)} %all_gather.26), kind=kOutput, calls=%fused_computation.50 | convolution fusion | flops 408944640 | bytes 2961920 | tf_op jit(solution)/shard_map/fh,xyhz->xyfz/dot_general | solution.py:145
  235.7 1.7 copy.623
  241.3 1.5 collective-permute-start.15
  243.6 4.6 collective-permute-done.15
  249.5 2.0 all_gather.30
  251.5 11.6 %collective-permute-done.20 = bf16[8,80,2,128]{3,1,2,0:T(8,128)(2,1)S(1)} collective-permute-done((bf16[8,80,2,128]{3,1,2,0:T(8,128)(2,1)S(1)}, bf16[8,80,2,128]{3,1,2,0:T(8,128)(2,1)S(1)}, u32[]{:S(2)}, u32[]{:S(2)}) %collective-permute-start.20) | collective-permute-done | bytes 327712 | tf_op jit(solution)/shard_map/ppermute | solution.py:13
  263.1 10.7 %collective-permute-done.21 = bf16[8,80,2,128]{3,1,2,0:T(8,128)(2,1)S(1)} collective-permute-done((bf16[8,80,2,128]{3,1,2,0:T(8,128)(2,1)S(1)}, bf16[8,80,2,128]{3,1,2,0:T(8,128)(2,1)S(1)}, u32[]{:S(2)}, u32[]{:S(2)}) %collective-permute-start.21) | collective-permute-done | bytes 327712 | tf_op jit(solution)/shard_map/ppermute | solution.py:13
  273.9 9.8 %collective-permute-done.22 = bf16[8,80,2,128]{3,1,2,0:T(8,128)(2,1)S(1)} collective-permute-done((bf16[8,80,2,128]{3,1,2,0:T(8,128)(2,1)S(1)}, bf16[8,80,2,128]{3,1,2,0:T(8,128)(2,1)S(1)}, u32[]{:S(2)}, u32[]{:S(2)}) %collective-permute-start.22) | collective-permute-done | bytes 327712 | tf_op jit(solution)/shard_map/ppermute | solution.py:13
  286.5 1.5 collective-permute-start.23
  288.0 5.7 %collective-permute-done.23 = bf16[16,40,2,128]{3,1,0,2:T(8,128)(2,1)S(1)} collective-permute-done((bf16[16,40,2,128]{3,1,0,2:T(8,128)(2,1)S(1)}, bf16[16,40,2,128]{3,1,0,2:T(8,128)(2,1)S(1)}, u32[]{:S(2)}, u32[]{:S(2)}) %collective-permute-start.23) | collective-permute-done | bytes 327712 | tf_op jit(solution)/shard_map/ppermute | solution.py:39
  295.1 1.5 collective-permute-start.24
  296.7 5.6 %collective-permute-done.24 = bf16[16,40,2,128]{3,1,0,2:T(8,128)(2,1)S(1)} collective-permute-done((bf16[16,40,2,128]{3,1,0,2:T(8,128)(2,1)S(1)}, bf16[16,40,2,128]{3,1,0,2:T(8,128)(2,1)S(1)}, u32[]{:S(2)}, u32[]{:S(2)}) %collective-permute-start.24) | collective-permute-done | bytes 327712 | tf_op jit(solution)/shard_map/ppermute | solution.py:39
  309.2 1.8 collective-permute-done.27
  313.6 22.6 %reduce-scatter.17.cloned.1.call-done = bf16[8,80,2,128]{3,1,2,0:T(8,128)(2,1)} async-done(((bf16[32,80,2,128]{3,1,2,0:T(8,128)(2,1)}), bf16[8,80,2,128]{3,1,2,0:T(8,128)(2,1)}) %reduce-scatter.17.cloned.1.call-update) | async-done | bytes 327696 | tf_op jit(solution)/shard_map/reduce_scatter | solution.py:155
  336.2 1.8 copy.338
  338.3 11.3 %fusion.18 = bf16[8,40,128,18]{2,3,1,0:T(8,128)(2,1)} fusion(f32[128]{0:T(128)S(1)} %copy-done.32, bf16[8,40,18,128]{3,1,2,0:T(8,128)(2,1)} %bitcast.657, bf16[4,18,128]{2,1,0:T(8,128)(2,1)} %copy-done.24, bf16[4,128,18]{1,2,0:T(8,128)(2,1)S(1)} %all_gather.26), kind=kOutput, calls=%fused_computation.49 | convolution fusion | flops 408944640 | bytes 2961920 | tf_op jit(solution)/shard_map/fh,xyhz->xyfz/dot_general | solution.py:145
  349.6 1.7 copy.624
  355.1 1.5 collective-permute-start.25
  357.5 4.6 collective-permute-done.25
  363.4 2.0 all_gather.31
  365.5 11.6 %collective-permute-done.30 = bf16[8,80,2,128]{3,1,2,0:T(8,128)(2,1)S(1)} collective-permute-done((bf16[8,80,2,128]{3,1,2,0:T(8,128)(2,1)S(1)}, bf16[8,80,2,128]{3,1,2,0:T(8,128)(2,1)S(1)}, u32[]{:S(2)}, u32[]{:S(2)}) %collective-permute-start.30) | collective-permute-done | bytes 327712 | tf_op jit(solution)/shard_map/ppermute | solution.py:13
  377.0 10.7 %collective-permute-done.31 = bf16[8,80,2,128]{3,1,2,0:T(8,128)(2,1)S(1)} collective-permute-done((bf16[8,80,2,128]{3,1,2,0:T(8,128)(2,1)S(1)}, bf16[8,80,2,128]{3,1,2,0:T(8,128)(2,1)S(1)}, u32[]{:S(2)}, u32[]{:S(2)}) %collective-permute-start.31) | collective-permute-done | bytes 327712 | tf_op jit(solution)/shard_map/ppermute | solution.py:13
  387.9 9.8 %collective-permute-done.32 = bf16[8,80,2,128]{3,1,2,0:T(8,128)(2,1)S(1)} collective-permute-done((bf16[8,80,2,128]{3,1,2,0:T(8,128)(2,1)S(1)}, bf16[8,80,2,128]{3,1,2,0:T(8,128)(2,1)S(1)}, u32[]{:S(2)}, u32[]{:S(2)}) %collective-permute-start.32) | collective-permute-done | bytes 327712 | tf_op jit(solution)/shard_map/ppermute | solution.py:13
  402.2 5.7 %collective-permute-done.33 = bf16[16,40,2,128]{3,1,0,2:T(8,128)(2,1)S(1)} collective-permute-done((bf16[16,40,2,128]{3,1,0,2:T(8,128)(2,1)S(1)}, bf16[16,40,2,128]{3,1,0,2:T(8,128)(2,1)S(1)}, u32[]{:S(2)}, u32[]{:S(2)}) %collective-permute-start.33) | collective-permute-done | bytes 327712 | tf_op jit(solution)/shard_map/ppermute | solution.py:39
  409.3 1.5 collective-permute-start.34
  410.9 5.6 %collective-permute-done.34 = bf16[16,40,2,128]{3,1,0,2:T(8,128)(2,1)S(1)} collective-permute-done((bf16[16,40,2,128]{3,1,0,2:T(8,128)(2,1)S(1)}, bf16[16,40,2,128]{3,1,0,2:T(8,128)(2,1)S(1)}, u32[]{:S(2)}, u32[]{:S(2)}) %collective-permute-start.34) | collective-permute-done | bytes 327712 | tf_op jit(solution)/shard_map/ppermute | solution.py:39
  422.1 1.6 collective-permute-start.37
  427.8 22.6 %reduce-scatter.21.cloned.1.call-done = bf16[8,80,2,128]{3,1,2,0:T(8,128)(2,1)} async-done(((bf16[32,80,2,128]{3,1,2,0:T(8,128)(2,1)}), bf16[8,80,2,128]{3,1,2,0:T(8,128)(2,1)}) %reduce-scatter.21.cloned.1.call-update) | async-done | bytes 327696 | tf_op jit(solution)/shard_map/reduce_scatter | solution.py:155
  450.4 1.8 copy.358
  452.2 11.3 %fusion.16 = bf16[8,40,128,18]{2,3,1,0:T(8,128)(2,1)} fusion(f32[128]{0:T(128)S(1)} %get-tuple-element.79, bf16[8,40,18,128]{3,1,2,0:T(8,128)(2,1)} %bitcast.654, bf16[4,18,128]{2,1,0:T(8,128)(2,1)} %copy-done.24, bf16[4,128,18]{1,2,0:T(8,128)(2,1)S(1)} %all_gather.26), kind=kOutput, calls=%fused_computation.48 | convolution fusion | flops 408944640 | bytes 2961920 | tf_op jit(solution)/shard_map/fh,xyhz->xyfz/dot_general | solution.py:145
  463.5 1.7 copy.625
  469.1 1.6 collective-permute-start.35
  471.5 4.6 collective-permute-done.35
  477.9 13.8 %all_to_all.12 = bf16[4,1,8,40,2,128]{5,4,3,2,1,0:T(2,128)(2,1)S(1)} all-to-all(bf16[4,1,8,40,2,128]{5,4,3,2,1,0:T(2,128)(2,1)S(1)} %copy.365), channel_id=1, replica_groups=mesh['section'=4,'coil'=4,'cuts'=2] {'section'}, dimensions={0} | all-to-all | bytes 1310720 | tf_op jit(solution)/shard_map/all_to_all | solution.py:266
  (320 shorter events, 89.6 us)
Async XLA Ops:
  6.5 16.5 %copy-start = (bf16[2,1,32,80,2,128]{5,4,3,2,1,0:T(2,128)(2,1)S(1)}, bf16[2,1,32,80,2,128]{5,4,3,2,1,0:T(2,128)(2,1)}, u32[]{:S(2)}) copy-start(bf16[2,1,32,80,2,128]{5,4,3,2,1,0:T(2,128)(2,1)} %param.11) | copy-start | bytes 7864324
  6.5 101.9 %reduce-scatter.9.cloned.1.call-start = ((), (), s32[]{:S(2)}) async-start(), calls=%async_computation.9 | async-start | bytes 1638400 | tf_op jit(solution)/shard_map/reduce_scatter | solution.py:155
  9.9 13.1 %collective-permute-start = (bf16[8,80,2,128]{3,1,2,0:T(8,128)(2,1)S(1)}, bf16[8,80,2,128]{3,1,2,0:T(8,128)(2,1)}, u32[]{:S(2)}, u32[]{:S(2)}) collective-permute-start(bf16[8,80,2,128]{3,1,2,0:T(8,128)(2,1)S(1)} %bitcast.658), channel_id=1, source_target_pairs={{0,2},{2,4},{4,6},{6,0},{1,3},{3,5},{5,7},{7,1},{8,10},{10,12},{12... | collective-permute-start | bytes 983048 | tf_op jit(solution)/shard_map/ppermute | solution.py:13
  23.0 11.3 %collective-permute-start.1 = (bf16[8,80,2,128]{3,1,2,0:T(8,128)(2,1)}, bf16[8,80,2,128]{3,1,2,0:T(8,128)(2,1)}, u32[]{:S(2)}, u32[]{:S(2)}) collective-permute-start(bf16[8,80,2,128]{3,1,2,0:T(8,128)(2,1)} %collective-permute-done), channel_id=1, source_target_pairs={{0,2},{2,4},{4,6},{6,0},{1,3},{3,5},{5,7},{7,1},{8,10},{10,12},{12... | collective-permute-start | bytes 983048 | tf_op jit(solution)/shard_map/ppermute | solution.py:13
  34.3 10.3 %collective-permute-start.2 = (bf16[8,80,2,128]{3,1,2,0:T(8,128)(2,1)}, bf16[8,80,2,128]{3,1,2,0:T(8,128)(2,1)S(1)}, u32[]{:S(2)}, u32[]{:S(2)}) collective-permute-start(bf16[8,80,2,128]{3,1,2,0:T(8,128)(2,1)} %collective-permute-done.1), channel_id=1, source_target_pairs={{0,2},{2,4},{4,6},{6,0},{1,3},{3,5},{5,7},{7,1},{8,10},{10,12},{12... | collective-permute-start | bytes 983048 | tf_op jit(solution)/shard_map/ppermute | solution.py:13
  34.9 11.5 %copy-start.10 = (bf16[128,128]{1,0:T(8,128)(2,1)}, bf16[128,128]{1,0:T(8,128)(2,1)S(1)}, u32[]{:S(2)}) copy-start(bf16[128,128]{1,0:T(8,128)(2,1)S(1)} %get-tuple-element.92) | copy-start | bytes 98308
  47.4 7.7 %collective-permute-start.3 = (bf16[16,40,2,128]{3,1,0,2:T(8,128)(2,1)S(1)}, bf16[16,40,2,128]{3,1,0,2:T(8,128)(2,1)S(1)}, u32[]{:S(2)}, u32[]{:S(2)}) collective-permute-start(bf16[16,40,2,128]{3,1,0,2:T(8,128)(2,1)S(1)} %dynamic-slice_bitcast_fusion.7), channel_id=1, source_target_pairs={{0,8},{8,0},{16,24},{24,16},{1,9},{9,1},{17,25},{25,17},{2,10},{10... | collective-permute-start | bytes 983048 | tf_op jit(solution)/shard_map/ppermute | solution.py:39
  56.4 7.1 %collective-permute-start.4 = (bf16[16,40,2,128]{3,1,0,2:T(8,128)(2,1)S(1)}, bf16[16,40,2,128]{3,1,0,2:T(8,128)(2,1)S(1)}, u32[]{:S(2)}, u32[]{:S(2)}) collective-permute-start(bf16[16,40,2,128]{3,1,0,2:T(8,128)(2,1)S(1)} %dynamic-slice_bitcast_fusion.6), channel_id=1, source_target_pairs={{0,8},{8,0},{16,24},{24,16},{1,9},{9,1},{17,25},{25,17},{2,10},{10... | collective-permute-start | bytes 983048 | tf_op jit(solution)/shard_map/ppermute | solution.py:39
  66.6 14.7 %copy-start.29 = (bf16[1,128,18]{1,2,0:T(8,128)(2,1)S(1)}, bf16[1,128,18]{1,2,0:T(8,128)(2,1)}, u32[]{:S(2)}) copy-start(bf16[1,128,18]{1,2,0:T(8,128)(2,1)} %param.15) | copy-start | bytes 13828
  66.6 31.8 %copy-start.30 = (bf16[1,18,128]{2,1,0:T(8,128)(2,1)S(1)}, bf16[1,18,128]{2,1,0:T(8,128)(2,1)}, u32[]{:S(2)}) copy-start(bf16[1,18,128]{2,1,0:T(8,128)(2,1)} %param.17) | copy-start | bytes 13828
  67.9 58.9 %reduce-scatter.11.cloned.1.call-start = ((), (), s32[]{:S(2)}) async-start(), calls=%async_computation.10 | async-start | bytes 491520 | tf_op jit(solution)/shard_map/reduce_scatter | solution.py:161
  67.9 37.9 %collective-permute-start.6 = (bf16[8,1,2,128]{3,1,2,0:T(2,128)(2,1)S(1)}, bf16[8,1,2,128]{3,1,2,0:T(2,128)(2,1)S(1)}, u32[]{:S(2)}, u32[]{:S(2)}) collective-permute-start(bf16[8,1,2,128]{3,1,2,0:T(2,128)(2,1)S(1)} %get-tuple-element.70), channel_id=1, source_target_pairs={{0,1},{2,3},{4,5},{6,7},{8,9},{10,11},{12,13},{14,15},{16,17},{18,... | collective-permute-start | bytes 12296 | tf_op jit(solution)/shard_map/ppermute | solution.py:26
  69.2 36.6 %collective-permute-start.7 = (bf16[8,1,2,128]{3,1,2,0:T(2,128)(2,1)S(1)}, bf16[8,1,2,128]{3,1,2,0:T(2,128)(2,1)S(1)}, u32[]{:S(2)}, u32[]{:S(2)}) collective-permute-start(bf16[8,1,2,128]{3,1,2,0:T(2,128)(2,1)S(1)} %get-tuple-element.71), channel_id=1, source_target_pairs={{1,0},{3,2},{5,4},{7,6},{9,8},{11,10},{13,12},{15,14},{17,16},{19,... | collective-permute-start | bytes 12296 | tf_op jit(solution)/shard_map/ppermute | solution.py:27
  110.3 111.7 %reduce-scatter.13.cloned.1.call-start = ((), (), s32[]{:S(2)}) async-start(), calls=%async_computation.11 | async-start | bytes 1638400 | tf_op jit(solution)/shard_map/reduce_scatter | solution.py:155
  123.5 5.8 %collective-permute-start.8 = (bf16[8,1,18,128]{3,1,2,0:T(2,128)(2,1)S(1)}, bf16[8,1,18,128]{3,1,2,0:T(2,128)(2,1)S(1)}, u32[]{:S(2)}, u32[]{:S(2)}) collective-permute-start(bf16[8,1,18,128]{3,1,2,0:T(2,128)(2,1)S(1)} %get-tuple-element.20), channel_id=1, source_target_pairs={{0,1},{2,3},{4,5},{6,7},{8,9},{10,11},{12,13},{14,15},{16,17},{18,... | collective-permute-start | bytes 110600 | tf_op jit(solution)/shard_map/ppermute | solution.py:26
  124.8 4.5 collective-permute-start.9
  127.8 7.0 %copy-start.2 = (bf16[8,40,2,128]{3,0,2,1:T(8,128)(2,1)S(1)}, bf16[8,40,2,128]{3,0,2,1:T(8,128)(2,1)}, u32[]{:S(2)}) copy-start(bf16[8,40,2,128]{3,0,2,1:T(8,128)(2,1)} %reduce-scatter.11.cloned.1.call-done) | copy-start | bytes 491524
  127.8 7.0 %collective-permute-start.5 = (bf16[8,40,2,128]{3,1,2,0:T(8,128)(2,1)S(1)}, bf16[8,40,2,128]{3,1,2,0:T(8,128)(2,1)S(1)}, u32[]{:S(2)}, u32[]{:S(2)}) collective-permute-start(bf16[8,40,2,128]{3,1,2,0:T(8,128)(2,1)S(1)} %copy.299), channel_id=1, source_target_pairs={{0,8},{8,0},{16,24},{24,16},{1,9},{9,1},{17,25},{25,17},{2,10},{10... | collective-permute-start | bytes 491528 | tf_op jit(solution)/shard_map/ppermute | solution.py:39
  138.0 11.6 %collective-permute-start.10 = (bf16[8,80,2,128]{3,1,2,0:T(8,128)(2,1)S(1)}, bf16[8,80,2,128]{3,1,2,0:T(8,128)(2,1)S(1)}, u32[]{:S(2)}, u32[]{:S(2)}) collective-permute-start(bf16[8,80,2,128]{3,1,2,0:T(8,128)(2,1)S(1)} %all_gather.29), channel_id=1, source_target_pairs={{0,2},{2,4},{4,6},{6,0},{1,3},{3,5},{5,7},{7,1},{8,10},{10,12},{12... | collective-permute-start | bytes 983048 | tf_op jit(solution)/shard_map/ppermute | solution.py:13
  149.6 10.7 %collective-permute-start.11 = (bf16[8,80,2,128]{3,1,2,0:T(8,128)(2,1)S(1)}, bf16[8,80,2,128]{3,1,2,0:T(8,128)(2,1)S(1)}, u32[]{:S(2)}, u32[]{:S(2)}) collective-permute-start(bf16[8,80,2,128]{3,1,2,0:T(8,128)(2,1)S(1)} %collective-permute-done.10), channel_id=1, source_target_pairs={{0,2},{2,4},{4,6},{6,0},{1,3},{3,5},{5,7},{7,1},{8,10},{10,12},{12... | collective-permute-start | bytes 983048 | tf_op jit(solution)/shard_map/ppermute | solution.py:13
  160.3 10.1 %collective-permute-start.12 = (bf16[8,80,2,128]{3,1,2,0:T(8,128)(2,1)S(1)}, bf16[8,80,2,128]{3,1,2,0:T(8,128)(2,1)S(1)}, u32[]{:S(2)}, u32[]{:S(2)}) collective-permute-start(bf16[8,80,2,128]{3,1,2,0:T(8,128)(2,1)S(1)} %collective-permute-done.11), channel_id=1, source_target_pairs={{0,2},{2,4},{4,6},{6,0},{1,3},{3,5},{5,7},{7,1},{8,10},{10,12},{12... | collective-permute-start | bytes 983048 | tf_op jit(solution)/shard_map/ppermute | solution.py:13
  173.3 7.5 %copy-start.7 = (bf16[1,1,32,40,2,128]{5,4,3,2,1,0:T(2,128)(2,1)S(1)}, bf16[1,1,32,40,2,128]{5,4,3,2,1,0:T(2,128)(2,1)}, u32[]{:S(2)}) copy-start(bf16[1,1,32,40,2,128]{5,4,3,2,1,0:T(2,128)(2,1)} %copy-done.6) | copy-start | bytes 1966084
  173.3 7.5 %copy-start.14 = (bf16[2,32,2,32,1]{1,3,0,4,2:T(8,128)(2,1)S(1)}, bf16[2,32,2,32,1]{1,3,0,4,2:T(8,128)(2,1)}, u32[]{:S(2)}) copy-start(bf16[2,32,2,32,1]{1,3,0,4,2:T(8,128)(2,1)} %copy-done.13) | copy-start | bytes 24580
  173.3 7.5 %copy-start.26 = (f32[40,128]{1,0:T(8,128)S(1)}, f32[40,128]{1,0:T(8,128)}, u32[]{:S(2)}) copy-start(f32[40,128]{1,0:T(8,128)} %copy-done.25) | copy-start | bytes 61444
  173.3 7.2 %collective-permute-start.13 = (bf16[16,40,2,128]{3,1,0,2:T(8,128)(2,1)S(1)}, bf16[16,40,2,128]{3,1,0,2:T(8,128)(2,1)S(1)}, u32[]{:S(2)}, u32[]{:S(2)}) collective-permute-start(bf16[16,40,2,128]{3,1,0,2:T(8,128)(2,1)S(1)} %dynamic-slice_bitcast_fusion.5), channel_id=1, source_target_pairs={{0,8},{8,0},{16,24},{24,16},{1,9},{9,1},{17,25},{25,17},{2,10},{10... | collective-permute-start | bytes 983048 | tf_op jit(solution)/shard_map/ppermute | solution.py:39
  181.9 7.1 %collective-permute-start.14 = (bf16[16,40,2,128]{3,1,0,2:T(8,128)(2,1)S(1)}, bf16[16,40,2,128]{3,1,0,2:T(8,128)(2,1)S(1)}, u32[]{:S(2)}, u32[]{:S(2)}) collective-permute-start(bf16[16,40,2,128]{3,1,0,2:T(8,128)(2,1)S(1)} %dynamic-slice_bitcast_fusion.4), channel_id=1, source_target_pairs={{0,8},{8,0},{16,24},{24,16},{1,9},{9,1},{17,25},{25,17},{2,10},{10... | collective-permute-start | bytes 983048 | tf_op jit(solution)/shard_map/ppermute | solution.py:39
  193.3 47.0 %reduce-scatter.15.cloned.1.call-start = ((), (), s32[]{:S(2)}) async-start(), calls=%async_computation.12 | async-start | bytes 491520 | tf_op jit(solution)/shard_map/reduce_scatter | solution.py:161
  193.4 2.6 collective-permute-start.16
  194.7 3.1 collective-permute-start.17
  199.0 25.5 %copy-start.33 = (f32[128]{0:T(128)S(1)}, f32[128]{0:T(128)}, u32[]{:S(2)}) copy-start(f32[128]{0:T(128)} %get-tuple-element.78) | copy-start | bytes 1540
  223.9 112.3 %reduce-scatter.17.cloned.1.call-start = ((), (), s32[]{:S(2)}) async-start(), calls=%async_computation.13 | async-start | bytes 1638400 | tf_op jit(solution)/shard_map/reduce_scatter | solution.py:155
  237.6 5.2 %collective-permute-start.18 = (bf16[8,1,18,128]{3,1,2,0:T(2,128)(2,1)S(1)}, bf16[8,1,18,128]{3,1,2,0:T(2,128)(2,1)S(1)}, u32[]{:S(2)}, u32[]{:S(2)}) collective-permute-start(bf16[8,1,18,128]{3,1,2,0:T(2,128)(2,1)S(1)} %get-tuple-element.18), channel_id=1, source_target_pairs={{0,1},{2,3},{4,5},{6,7},{8,9},{10,11},{12,13},{14,15},{16,17},{18,... | collective-permute-start | bytes 110600 | tf_op jit(solution)/shard_map/ppermute | solution.py:26
  239.0 3.8 collective-permute-start.19
  241.3 7.0 %collective-permute-start.15 = (bf16[8,40,2,128]{3,1,2,0:T(8,128)(2,1)S(1)}, bf16[8,40,2,128]{3,1,2,0:T(8,128)(2,1)S(1)}, u32[]{:S(2)}, u32[]{:S(2)}) collective-permute-start(bf16[8,40,2,128]{3,1,2,0:T(8,128)(2,1)S(1)} %copy.319), channel_id=1, source_target_pairs={{0,8},{8,0},{16,24},{24,16},{1,9},{9,1},{17,25},{25,17},{2,10},{10... | collective-permute-start | bytes 491528 | tf_op jit(solution)/shard_map/ppermute | solution.py:39
  251.5 11.6 %collective-permute-start.20 = (bf16[8,80,2,128]{3,1,2,0:T(8,128)(2,1)S(1)}, bf16[8,80,2,128]{3,1,2,0:T(8,128)(2,1)S(1)}, u32[]{:S(2)}, u32[]{:S(2)}) collective-permute-start(bf16[8,80,2,128]{3,1,2,0:T(8,128)(2,1)S(1)} %all_gather.30), channel_id=1, source_target_pairs={{0,2},{2,4},{4,6},{6,0},{1,3},{3,5},{5,7},{7,1},{8,10},{10,12},{12... | collective-permute-start | bytes 983048 | tf_op jit(solution)/shard_map/ppermute | solution.py:13
  263.1 10.7 %collective-permute-start.21 = (bf16[8,80,2,128]{3,1,2,0:T(8,128)(2,1)S(1)}, bf16[8,80,2,128]{3,1,2,0:T(8,128)(2,1)S(1)}, u32[]{:S(2)}, u32[]{:S(2)}) collective-permute-start(bf16[8,80,2,128]{3,1,2,0:T(8,128)(2,1)S(1)} %collective-permute-done.20), channel_id=1, source_target_pairs={{0,2},{2,4},{4,6},{6,0},{1,3},{3,5},{5,7},{7,1},{8,10},{10,12},{12... | collective-permute-start | bytes 983048 | tf_op jit(solution)/shard_map/ppermute | solution.py:13
  273.8 10.0 %collective-permute-start.22 = (bf16[8,80,2,128]{3,1,2,0:T(8,128)(2,1)S(1)}, bf16[8,80,2,128]{3,1,2,0:T(8,128)(2,1)S(1)}, u32[]{:S(2)}, u32[]{:S(2)}) collective-permute-start(bf16[8,80,2,128]{3,1,2,0:T(8,128)(2,1)S(1)} %collective-permute-done.21), channel_id=1, source_target_pairs={{0,2},{2,4},{4,6},{6,0},{1,3},{3,5},{5,7},{7,1},{8,10},{10,12},{12... | collective-permute-start | bytes 983048 | tf_op jit(solution)/shard_map/ppermute | solution.py:13
  286.5 7.5 %copy-start.8 = (bf16[1,1,32,40,2,128]{5,4,3,2,1,0:T(2,128)(2,1)S(1)}, bf16[1,1,32,40,2,128]{5,4,3,2,1,0:T(2,128)(2,1)}, u32[]{:S(2)}) copy-start(bf16[1,1,32,40,2,128]{5,4,3,2,1,0:T(2,128)(2,1)} %copy-done.6) | copy-start | bytes 1966084
  286.5 7.5 %copy-start.27 = (f32[40,128]{1,0:T(8,128)S(1)}, f32[40,128]{1,0:T(8,128)}, u32[]{:S(2)}) copy-start(f32[40,128]{1,0:T(8,128)} %copy-done.25) | copy-start | bytes 61444
  286.5 7.3 %collective-permute-start.23 = (bf16[16,40,2,128]{3,1,0,2:T(8,128)(2,1)S(1)}, bf16[16,40,2,128]{3,1,0,2:T(8,128)(2,1)S(1)}, u32[]{:S(2)}, u32[]{:S(2)}) collective-permute-start(bf16[16,40,2,128]{3,1,0,2:T(8,128)(2,1)S(1)} %dynamic-slice_bitcast_fusion.3), channel_id=1, source_target_pairs={{0,8},{8,0},{16,24},{24,16},{1,9},{9,1},{17,25},{25,17},{2,10},{10... | collective-permute-start | bytes 983048 | tf_op jit(solution)/shard_map/ppermute | solution.py:39
  295.1 7.1 %collective-permute-start.24 = (bf16[16,40,2,128]{3,1,0,2:T(8,128)(2,1)S(1)}, bf16[16,40,2,128]{3,1,0,2:T(8,128)(2,1)S(1)}, u32[]{:S(2)}, u32[]{:S(2)}) collective-permute-start(bf16[16,40,2,128]{3,1,0,2:T(8,128)(2,1)S(1)} %dynamic-slice_bitcast_fusion.2), channel_id=1, source_target_pairs={{0,8},{8,0},{16,24},{24,16},{1,9},{9,1},{17,25},{25,17},{2,10},{10... | collective-permute-start | bytes 983048 | tf_op jit(solution)/shard_map/ppermute | solution.py:39
  306.5 47.6 %reduce-scatter.19.cloned.1.call-start = ((), (), s32[]{:S(2)}) async-start(), calls=%async_computation.14 | async-start | bytes 491520 | tf_op jit(solution)/shard_map/reduce_scatter | solution.py:161
  306.6 2.6 collective-permute-start.26
  307.9 3.1 collective-permute-start.27
  312.2 26.1 %copy-start.32 = (f32[128]{0:T(128)S(1)}, f32[128]{0:T(128)}, u32[]{:S(2)}) copy-start(f32[128]{0:T(128)} %get-tuple-element.77) | copy-start | bytes 1540
  338.1 112.3 %reduce-scatter.21.cloned.1.call-start = ((), (), s32[]{:S(2)}) async-start(), calls=%async_computation.15 | async-start | bytes 1638400 | tf_op jit(solution)/shard_map/reduce_scatter | solution.py:155
  351.5 5.2 %collective-permute-start.28 = (bf16[8,1,18,128]{3,1,2,0:T(2,128)(2,1)S(1)}, bf16[8,1,18,128]{3,1,2,0:T(2,128)(2,1)S(1)}, u32[]{:S(2)}, u32[]{:S(2)}) collective-permute-start(bf16[8,1,18,128]{3,1,2,0:T(2,128)(2,1)S(1)} %get-tuple-element.16), channel_id=1, source_target_pairs={{0,1},{2,3},{4,5},{6,7},{8,9},{10,11},{12,13},{14,15},{16,17},{18,... | collective-permute-start | bytes 110600 | tf_op jit(solution)/shard_map/ppermute | solution.py:26
  352.8 3.8 collective-permute-start.29
  355.1 7.0 %collective-permute-start.25 = (bf16[8,40,2,128]{3,1,2,0:T(8,128)(2,1)S(1)}, bf16[8,40,2,128]{3,1,2,0:T(8,128)(2,1)S(1)}, u32[]{:S(2)}, u32[]{:S(2)}) collective-permute-start(bf16[8,40,2,128]{3,1,2,0:T(8,128)(2,1)S(1)} %copy.339), channel_id=1, source_target_pairs={{0,8},{8,0},{16,24},{24,16},{1,9},{9,1},{17,25},{25,17},{2,10},{10... | collective-permute-start | bytes 491528 | tf_op jit(solution)/shard_map/ppermute | solution.py:39
  365.5 11.6 %collective-permute-start.30 = (bf16[8,80,2,128]{3,1,2,0:T(8,128)(2,1)S(1)}, bf16[8,80,2,128]{3,1,2,0:T(8,128)(2,1)S(1)}, u32[]{:S(2)}, u32[]{:S(2)}) collective-permute-start(bf16[8,80,2,128]{3,1,2,0:T(8,128)(2,1)S(1)} %all_gather.31), channel_id=1, source_target_pairs={{0,2},{2,4},{4,6},{6,0},{1,3},{3,5},{5,7},{7,1},{8,10},{10,12},{12... | collective-permute-start | bytes 983048 | tf_op jit(solution)/shard_map/ppermute | solution.py:13
  377.0 10.7 %collective-permute-start.31 = (bf16[8,80,2,128]{3,1,2,0:T(8,128)(2,1)S(1)}, bf16[8,80,2,128]{3,1,2,0:T(8,128)(2,1)S(1)}, u32[]{:S(2)}, u32[]{:S(2)}) collective-permute-start(bf16[8,80,2,128]{3,1,2,0:T(8,128)(2,1)S(1)} %collective-permute-done.30), channel_id=1, source_target_pairs={{0,2},{2,4},{4,6},{6,0},{1,3},{3,5},{5,7},{7,1},{8,10},{10,12},{12... | collective-permute-start | bytes 983048 | tf_op jit(solution)/shard_map/ppermute | solution.py:13
  387.7 10.1 %collective-permute-start.32 = (bf16[8,80,2,128]{3,1,2,0:T(8,128)(2,1)S(1)}, bf16[8,80,2,128]{3,1,2,0:T(8,128)(2,1)S(1)}, u32[]{:S(2)}, u32[]{:S(2)}) collective-permute-start(bf16[8,80,2,128]{3,1,2,0:T(8,128)(2,1)S(1)} %collective-permute-done.31), channel_id=1, source_target_pairs={{0,2},{2,4},{4,6},{6,0},{1,3},{3,5},{5,7},{7,1},{8,10},{10,12},{12... | collective-permute-start | bytes 983048 | tf_op jit(solution)/shard_map/ppermute | solution.py:13
  400.7 7.5 %copy-start.9 = (bf16[1,1,32,40,2,128]{5,4,3,2,1,0:T(2,128)(2,1)S(1)}, bf16[1,1,32,40,2,128]{5,4,3,2,1,0:T(2,128)(2,1)}, u32[]{:S(2)}) copy-start(bf16[1,1,32,40,2,128]{5,4,3,2,1,0:T(2,128)(2,1)} %copy-done.6) | copy-start | bytes 1966084
  400.7 7.5 %copy-start.15 = (bf16[2,32,2,32,1]{1,3,0,4,2:T(8,128)(2,1)S(1)}, bf16[2,32,2,32,1]{1,3,0,4,2:T(8,128)(2,1)}, u32[]{:S(2)}) copy-start(bf16[2,32,2,32,1]{1,3,0,4,2:T(8,128)(2,1)} %copy-done.13) | copy-start | bytes 24580
  400.7 7.5 %copy-start.28 = (f32[40,128]{1,0:T(8,128)S(1)}, f32[40,128]{1,0:T(8,128)}, u32[]{:S(2)}) copy-start(f32[40,128]{1,0:T(8,128)} %copy-done.25) | copy-start | bytes 61444
  400.7 7.3 %collective-permute-start.33 = (bf16[16,40,2,128]{3,1,0,2:T(8,128)(2,1)S(1)}, bf16[16,40,2,128]{3,1,0,2:T(8,128)(2,1)S(1)}, u32[]{:S(2)}, u32[]{:S(2)}) collective-permute-start(bf16[16,40,2,128]{3,1,0,2:T(8,128)(2,1)S(1)} %dynamic-slice_bitcast_fusion.1), channel_id=1, source_target_pairs={{0,8},{8,0},{16,24},{24,16},{1,9},{9,1},{17,25},{25,17},{2,10},{10... | collective-permute-start | bytes 983048 | tf_op jit(solution)/shard_map/ppermute | solution.py:39
  409.3 7.1 %collective-permute-start.34 = (bf16[16,40,2,128]{3,1,0,2:T(8,128)(2,1)S(1)}, bf16[16,40,2,128]{3,1,0,2:T(8,128)(2,1)S(1)}, u32[]{:S(2)}, u32[]{:S(2)}) collective-permute-start(bf16[16,40,2,128]{3,1,0,2:T(8,128)(2,1)S(1)} %dynamic-slice_bitcast_fusion), channel_id=1, source_target_pairs={{0,8},{8,0},{16,24},{24,16},{1,9},{9,1},{17,25},{25,17},{2,10},{10... | collective-permute-start | bytes 983048 | tf_op jit(solution)/shard_map/ppermute | solution.py:39
  420.8 47.3 %reduce-scatter.23.cloned.1.call-start = ((), (), s32[]{:S(2)}) async-start(), calls=%async_computation.16 | async-start | bytes 491520 | tf_op jit(solution)/shard_map/reduce_scatter | solution.py:161
  420.8 2.9 collective-permute-start.36
  422.1 3.1 collective-permute-start.37
  465.4 5.2 %collective-permute-start.38 = (bf16[8,1,18,128]{3,1,2,0:T(2,128)(2,1)S(1)}, bf16[8,1,18,128]{3,1,2,0:T(2,128)(2,1)S(1)}, u32[]{:S(2)}, u32[]{:S(2)}) collective-permute-start(bf16[8,1,18,128]{3,1,2,0:T(2,128)(2,1)S(1)} %get-tuple-element.14), channel_id=1, source_target_pairs={{0,1},{2,3},{4,5},{6,7},{8,9},{10,11},{12,13},{14,15},{16,17},{18,... | collective-permute-start | bytes 110600 | tf_op jit(solution)/shard_map/ppermute | solution.py:26
  466.8 3.9 collective-permute-start.39
  469.1 7.0 %collective-permute-start.35 = (bf16[8,40,2,128]{3,1,2,0:T(8,128)(2,1)S(1)}, bf16[8,40,2,128]{3,1,2,0:T(8,128)(2,1)S(1)}, u32[]{:S(2)}, u32[]{:S(2)}) collective-permute-start(bf16[8,40,2,128]{3,1,2,0:T(8,128)(2,1)S(1)} %copy.359), channel_id=1, source_target_pairs={{0,8},{8,0},{16,24},{24,16},{1,9},{9,1},{17,25},{25,17},{2,10},{10... | collective-permute-start | bytes 491528 | tf_op jit(solution)/shard_map/ppermute | solution.py:39
  477.3 15.4 %copy-start.1 = (bf16[2,1,32,80,2,128]{5,4,3,2,1,0:T(2,128)(2,1)S(1)}, bf16[2,1,32,80,2,128]{5,4,3,2,1,0:T(2,128)(2,1)}, u32[]{:S(2)}) copy-start(bf16[2,1,32,80,2,128]{5,4,3,2,1,0:T(2,128)(2,1)} %param.11) | copy-start | bytes 7864324
  (19 other events, 69.3 us)
Sparse Core Ops, SparseCore 0:
  68.0 29.8 reduce-scatter.8
  110.4 4.9 reduce-scatter.10
  193.4 28.5 reduce-scatter.12
  224.1 6.4 reduce-scatter.14
  306.7 29.4 reduce-scatter.16
  338.3 6.4 reduce-scatter.18
  420.9 29.4 reduce-scatter.20
  452.6 6.4 reduce-scatter.22
